TPU v7x, 256 devices: a whole 4x4x8 slice. The times are simulated.
256 devices in a mesh: section: 2 (over core), seq: 64 (over z, y_hi, x), mp: 2 (over y_lo).
Axes of the slice: x: 4, y: 4 (y_hi: 2, y_lo: 2; y = y_hi * 2 + y_lo), z: 8, core: 2. Of those that a mesh axis runs over, the one named last changes fastest.
Arguments:
- patches: bfloat16 [32768, 1280], P(('section', 'seq')), may hold values from -6 to 6
- inner_weight: bfloat16 [3, 1280, 1280], P(None, None, 'mp'), may hold values from -0.15625 to 0.15625
- norm_gain: float32 [1280], replicated, may hold values from 0.5 to 12
- outer_weight: bfloat16 [1280, 1280], P('mp'), may hold values from -0.15625 to 0.15625
- merge_gain: float32 [1280], replicated, may hold values from 0.5 to 1.5
- windows: int32 [128, 256], P(('section', 'seq')), may hold values from 0 to 7, never falling along the last dimension, each value on 1 to 64 neighbouring positions
- owners: int32 [8192, 1], P(('section', 'seq')), may hold values from 0 to 127; in each aligned block of 64 rows (0 to 63, 64 to 127, ...) at most 2 rows name the same one
- context_query: bfloat16 [8192, 8192], P('seq', ('section', 'mp')), may hold values from -150 to 150
- context_key: bfloat16 [8192, 1024], P('seq', ('section', 'mp')), may hold values from -6 to 6
- context_value: bfloat16 [8192, 1024], P('seq', ('section', 'mp')), may hold values from -6 to 6
- documents: int32 [8192], replicated, may hold values from 0 to 7, never falling along the last dimension, each value on 1 to 6144 neighbouring positions
Outputs:
- delivered: bfloat16 [32768, 5120], P(('section', 'seq'), 'mp')
- attended: bfloat16 [8192, 8192], P('seq', ('section', 'mp'))
Inputs may be any that keep to these rules, and one draw needn't show every extreme that they name: Along each row the window numbers never fall, and each of the 8 windows holds 1 to 64 patches. `owners`: among the 64 tokens of one device (aligned blocks of rows) no owner is named more than 2 times; some owner is named exactly 2 times in some blocks. Document numbers never fall; each of the 8 documents holds 1 to 6144 positions, one exactly 6144.
All inputs are finite; a program needn't handle non-finite values.
Results may differ from a plain program's by a relative error of at most 0.012.
The roundings to bfloat16 on the way count: a program that leaves them out, or rounds other values in their place, can miss the bound.
Values may be sent and summed in bfloat16 or wider, within the bound.
No kernel may reach another device: no remote copies, remote signals or barrier semaphores. Data moves between devices by JAX's collectives and lax.ppermute only.
A program may use at most 128 MiB of HBM per device.

v0:
```python
import math

import jax
import jax.numpy as jnp
from jax import lax
from jax.sharding import PartitionSpec as P

VD = 1280
VH = 16
QH = 64
KVH = 8
HD = 128


EPSILON = 1e-06


def cut_along(x, dim, size):
    shape = x.shape
    tiles = x.reshape(*shape[:dim], size, shape[dim] // size, *shape[dim + 1 :])
    return jnp.moveaxis(tiles, dim, 0)


def sum_at_owner(x, axis, dim):
    tiles = cut_along(x, dim, lax.axis_size(axis))
    arrived = lax.all_to_all(tiles, axis, split_axis=0, concat_axis=0, tiled=True)
    return arrived.astype(jnp.float32).sum(axis=0)


def side_by_side(arrays, axis, dim, along):
    widths = [a.shape[along] for a in arrays]
    both = jnp.concatenate(arrays, axis=along)
    result = lax.all_gather(both, axis, axis=dim, tiled=True)
    return tuple(jnp.split(result, [sum(widths[:k]) for k in range(1, len(widths))], axis=along))


def rms_scale(values, gain):
    return values * lax.rsqrt(jnp.mean(values * values, axis=-1, keepdims=True) + EPSILON) * gain


def vision_part(patches, inner_weight, norm_gain, outer_weight, merge_gain, windows):
    patch_rows, feature_width = patches.shape
    head_dim = VD // VH
    local_heads = inner_weight.shape[2] // head_dim
    source = patches.astype(jnp.float32)
    normed = rms_scale(source, norm_gain).astype(jnp.bfloat16)
    query_heads = (
        jnp.dot(normed, inner_weight[0], preferred_element_type=jnp.float32)
        .astype(jnp.bfloat16)
        .reshape(patch_rows, local_heads, head_dim)
    )
    key_heads = (
        jnp.dot(normed, inner_weight[1], preferred_element_type=jnp.float32)
        .astype(jnp.bfloat16)
        .reshape(patch_rows, local_heads, head_dim)
    )
    value_heads = (
        jnp.dot(normed, inner_weight[2], preferred_element_type=jnp.float32)
        .astype(jnp.bfloat16)
        .reshape(patch_rows, local_heads, head_dim)
    )
    scores = jnp.einsum(
        "qhd,khd->hqk", query_heads, key_heads, preferred_element_type=jnp.float32
    ) / math.sqrt(head_dim)
    window_row = windows[0]
    allowed = window_row[:, None] == window_row[None, :]
    scores = jnp.where(allowed[None], scores, -jnp.inf)
    row_peak = jnp.max(scores, axis=-1, keepdims=True)
    weights = jnp.exp(scores - row_peak)
    denominator = jnp.sum(weights, axis=-1)
    context = jnp.einsum(
        "hqk,khd->qhd",
        weights.astype(jnp.bfloat16),
        value_heads,
        preferred_element_type=jnp.float32,
    )
    context = (
        (context / jnp.transpose(denominator)[:, :, None])
        .astype(jnp.bfloat16)
        .reshape(patch_rows, local_heads * head_dim)
    )
    partial_value = jnp.dot(context, outer_weight, preferred_element_type=jnp.float32)
    tokens = patch_rows // 4
    half_count = 4 // lax.axis_size("mp")
    first_patch = lax.axis_index("mp") * half_count
    summed = sum_at_owner(
        partial_value.reshape(tokens, 4, feature_width).astype(jnp.bfloat16), "mp", 1
    )
    residual = (
        lax.dynamic_slice_in_dim(
            source.reshape(tokens, 4, feature_width), first_patch, half_count, 1
        )
        + summed
    )
    merged = rms_scale(residual, merge_gain).astype(jnp.bfloat16)
    return merged.reshape(tokens, half_count * feature_width)


def deliver_tokens(merged, owners):
    tokens = merged.shape[0]
    owner_count = lax.axis_size(("section", "seq"))
    capacity = max(2, 4 * tokens // owner_count)
    target = owners[:, 0]
    order = jnp.arange(tokens, dtype=jnp.int32)
    earlier = (target[:, None] == target[None, :]) & (order[None, :] < order[:, None])
    slot_rank = jnp.sum(earlier, axis=1)
    slot_index = target * capacity + slot_rank
    outgoing = (
        jnp.zeros((owner_count * capacity, merged.shape[1]), jnp.bfloat16)
        .at[slot_index]
        .set(merged)
    )
    sections = lax.axis_size("section")
    arrived = lax.all_to_all(
        lax.all_to_all(
            outgoing.reshape(sections, owner_count // sections, capacity, merged.shape[1]),
            "seq",
            split_axis=1,
            concat_axis=1,
            tiled=True,
        ),
        "section",
        split_axis=0,
        concat_axis=0,
        tiled=True,
    )
    return arrived.reshape(owner_count * capacity, merged.shape[1])


def context_part(context_query, context_key, context_value, documents):
    query_rows = context_query.shape[0]
    kv_heads = context_key.shape[1] // HD
    groups = QH // KVH
    score_scale = 1.0 / math.sqrt(HD)
    query_heads = (
        context_query.reshape(query_rows, kv_heads, groups, HD)
        .transpose(1, 0, 2, 3)
        .reshape(kv_heads, query_rows * groups, HD)
    )
    first_position = lax.axis_index("seq") * query_rows
    query_positions = first_position + jnp.arange(query_rows, dtype=jnp.int32)
    query_docs = lax.dynamic_slice_in_dim(documents, first_position, query_rows, 0)
    row_positions = jnp.repeat(query_positions, groups)
    row_docs = jnp.repeat(query_docs, groups)

    def attend_block(running, key_block, value_block, key_positions, key_docs):
        row_peak, denominator, numerator = running
        scores = (
            jnp.einsum("hrd,khd->hrk", query_heads, key_block, preferred_element_type=jnp.float32)
            * score_scale
        )
        allowed = (key_positions[None, :] <= row_positions[:, None]) & (
            key_docs[None, :] == row_docs[:, None]
        )
        scores = jnp.where(allowed[None], scores, -1e30)
        new_peak = jnp.maximum(row_peak, jnp.max(scores, axis=-1))
        weights = jnp.where(allowed[None], jnp.exp(scores - new_peak[..., None]), 0.0)
        factor = jnp.exp(row_peak - new_peak)
        denominator = denominator * factor + jnp.sum(weights, axis=-1)
        numerator = numerator * factor[..., None] + jnp.einsum(
            "hrk,khd->hrd",
            weights.astype(jnp.bfloat16),
            value_block,
            preferred_element_type=jnp.float32,
        )
        return (new_peak, denominator, numerator)

    start_state = (
        jnp.full((kv_heads, query_rows * groups), -1e30, jnp.float32),
        jnp.zeros((kv_heads, query_rows * groups), jnp.float32),
        jnp.zeros((kv_heads, query_rows * groups, HD), jnp.float32),
    )
    key_local = context_key.reshape(query_rows, kv_heads, HD)
    value_local = context_value.reshape(query_rows, kv_heads, HD)
    key_piece, value_piece = side_by_side((key_local, value_local), "seq", 0, 1)
    piece_rows = key_piece.shape[0]
    block_size = math.gcd(piece_rows, 512)
    block_count = piece_rows // block_size
    key_blocks = key_piece.reshape(block_count, block_size, kv_heads, HD)
    value_blocks = value_piece.reshape(block_count, block_size, kv_heads, HD)

    def one_step(carry_state, inputs):
        block_index, key_block, value_block = inputs
        block_start = block_index * block_size
        key_positions = block_start + jnp.arange(block_size, dtype=jnp.int32)
        key_docs = lax.dynamic_slice_in_dim(documents, block_start, block_size, 0)
        return (attend_block(carry_state, key_block, value_block, key_positions, key_docs), None)

    row_peak, denominator, numerator = lax.scan(
        one_step, start_state, (jnp.arange(block_count, dtype=jnp.int32), key_blocks, value_blocks)
    )[0]
    output = (numerator / denominator[..., None]).astype(jnp.bfloat16)
    return (
        output.reshape(kv_heads, query_rows, groups, HD)
        .transpose(1, 0, 2, 3)
        .reshape(query_rows, kv_heads * groups * HD)
    )


def per_device(
    patches,
    inner_weight,
    norm_gain,
    outer_weight,
    merge_gain,
    windows,
    owners,
    context_query,
    context_key,
    context_value,
    documents,
):
    merged = vision_part(patches, inner_weight, norm_gain, outer_weight, merge_gain, windows)
    delivered = deliver_tokens(merged, owners)
    attended = context_part(context_query, context_key, context_value, documents)
    return (delivered, attended)


def solution(mesh):
    in_specs = (
        P(("section", "seq"), None),
        P(None, None, "mp"),
        P(),
        P("mp", None),
        P(),
        P(("section", "seq"), None),
        P(("section", "seq"), None),
        P("seq", ("section", "mp")),
        P("seq", ("section", "mp")),
        P("seq", ("section", "mp")),
        P(),
    )
    out_specs = (P(("section", "seq"), "mp"), P("seq", ("section", "mp")))
    return jax.shard_map(
        per_device, mesh=mesh, in_specs=in_specs, out_specs=out_specs, check_vma=False
    )
```

profile of v0, /device:TPU:8, one launch (start us, length us, event | category | flops | bytes accessed | tf_op | source)
XLA Modules:
  0.0 336.1 jit_solution(6429944411530990273)
XLA Ops:
  11.3 2.4 fusion.43
  13.9 2.2 fusion.46
  16.3 2.9 fusion.40
  26.2 5.7 %all-to-all-start = ((bf16[2,64,2,1280]{3,1,2,0:T(8,128)(2,1)}), bf16[2,64,2,1280]{3,1,2,0:T(8,128)(2,1)S(1)}, u32[]{:S(2)}, u32[]{:S(2)}) async-start(bf16[2,64,2,1280]{3,1,2,0:T(8,128)(2,1)} %bitcast.14), calls=%async_computation | async-start | bytes 1310720 | tf_op jit(solution)/shard_map/all_to_all | solution.py:26
  35.0 2.5 all-to-all-done
  40.9 3.4 %copy.109 = bf16[2,64,2,2560]{3,2,0,1:T(2,128)(2,1)} copy(bf16[2,64,2,2560]{3,2,1,0:T(2,128)(2,1)} %reshape.183) | data formatting | bytes 2621440 | tf_op jit(solution)/shard_map/reshape | solution.py:116
  44.4 14.5 %all-to-all-start.1 = ((bf16[2,64,2,2560]{3,2,0,1:T(2,128)(2,1)}), bf16[2,64,2,2560]{3,2,0,1:T(2,128)(2,1)S(1)}, u32[]{:S(2)}, u32[]{:S(2)}) async-start(bf16[2,64,2,2560]{3,2,0,1:T(2,128)(2,1)} %copy.109), calls=%async_computation.1 | async-start | bytes 2621440 | tf_op jit(solution)/shard_map/all_to_all | solution.py:115
  59.9 40.6 %all-to-all-done.1 = bf16[2,64,2,2560]{3,2,0,1:T(2,128)(2,1)S(1)} async-done(((bf16[2,64,2,2560]{3,2,0,1:T(2,128)(2,1)}), bf16[2,64,2,2560]{3,2,0,1:T(2,128)(2,1)S(1)}, u32[]{:S(2)}, u32[]{:S(2)}) %all-to-all-start.1) | async-done | bytes 1310752 | tf_op jit(solution)/shard_map/all_to_all | solution.py:115
  101.4 4.8 %all_to_all.15 = bf16[2,64,2,2560]{3,2,1,0:T(2,128)(2,1)S(1)} all-to-all(bf16[2,64,2,2560]{3,2,1,0:T(2,128)(2,1)S(1)} %copy.110), channel_id=1, replica_groups=mesh['section'=2,'seq'=64,'mp'=2] {'section'}, dimensions={0} | all-to-all | bytes 2621440 | tf_op jit(solution)/shard_map/all_to_all | solution.py:114
  107.5 54.7 %all-gather.2.cloned.1.call-done = bf16[8192,4,128]{0,2,1:T(8,128)(2,1)} async-done(((bf16[128,4,128]{0,2,1:T(8,128)(2,1)}), bf16[8192,4,128]{0,2,1:T(8,128)(2,1)}) %all-gather.2.cloned.1.call-update) | async-done | bytes 8388624 | tf_op jit(solution)/shard_map/all_gather | solution.py:33
  162.2 5.9 %fusion.63 = (bf16[8192,2,128]{0,2,1:T(8,128)(2,1)}, bf16[8192,2,128]{0,2,1:T(8,128)(2,1)}) fusion(bf16[8192,4,128]{0,2,1:T(8,128)(2,1)} %all-gather.2.cloned.1.call-done), kind=kLoop, calls=%fused_computation.83 | loop fusion | bytes 16777216 | tf_op jit(solution)/shard_map/split | solution.py:34
  168.1 6.4 %copy.115 = bf16[8192,2,128]{2,0,1:T(8,128)(2,1)} copy(bf16[8192,2,128]{0,2,1:T(8,128)(2,1)} %get-tuple-element.196) | data formatting | bytes 8388608 | tf_op jit(solution)/shard_map/split | solution.py:34
  174.5 6.4 %copy.113 = bf16[8192,2,128]{2,0,1:T(8,128)(2,1)} copy(bf16[8192,2,128]{0,2,1:T(8,128)(2,1)} %get-tuple-element.197) | data formatting | bytes 8388608 | tf_op jit(solution)/shard_map/split | solution.py:34
  180.9 147.0 %while.15 = (s32[]{:T(128)}, f32[2,1024]{1,0:T(2,128)S(1)}, f32[2,1024]{1,0:T(2,128)S(1)}, f32[2,1024,128]{2,1,0:T(8,128)S(1)}, s32[16]{0:T(128)S(1)}, /*index=5...) while((s32[]{:T(128)}, f32[2,1024]{1,0:T(2,128)S(1)}, ...), condition=%wide.region_10.11_spmd.clone, body=%wide.region_7.10_spmd.clone.sunk | while | flops 552872448 | bytes 18001132 | solution.py:189
  186.8 3.3 fusion.83
  192.9 2.0 fusion.79
  196.0 3.3 fusion.83
  202.1 2.0 fusion.79
  205.2 3.3 fusion.83
  214.4 3.3 fusion.83
  223.6 3.3 fusion.83
  232.7 3.3 fusion.83
  241.9 3.3 fusion.83
  251.1 3.3 fusion.83
  260.3 3.3 fusion.83
  269.5 3.3 fusion.83
  278.7 3.3 fusion.83
  287.9 3.3 fusion.83
  297.1 3.3 fusion.83
  306.2 3.3 fusion.83
  315.4 3.3 fusion.83
  324.6 3.3 fusion.83
  (263 shorter events, 102.7 us)
Async XLA Ops:
  7.2 17.4 %copy-start = (bf16[640,1280]{1,0:T(8,128)(2,1)S(1)}, bf16[640,1280]{1,0:T(8,128)(2,1)}, u32[]{:S(2)}) copy-start(bf16[640,1280]{1,0:T(8,128)(2,1)} %param.16) | copy-start | bytes 4915204
  7.2 155.1 %all-gather.2.cloned.1.call-start = ((), (), s32[]{:S(2)}) async-start(), calls=%async_computation.3 | async-start | bytes 8519680 | tf_op jit(solution)/shard_map/all_gather | solution.py:33
  11.3 2.6 copy-start.1
  11.3 2.6 copy-start.6
  16.3 4.0 %copy-start.5 = (s32[1,256]{1,0:T(1,128)S(1)}, s32[1,256]{1,0:T(1,128)}, u32[]{:S(2)}) copy-start(s32[1,256]{1,0:T(1,128)} %param.18) | copy-start | bytes 3076
  24.6 7.3 %copy-start.7 = (s32[64,1]{0,1:T(1,128)S(1)}, s32[64,1]{0,1:T(1,128)}, u32[]{:S(2)}) copy-start(s32[64,1]{0,1:T(1,128)} %param.19) | copy-start | bytes 772
  26.2 11.3 %all-to-all-start = ((bf16[2,64,2,1280]{3,1,2,0:T(8,128)(2,1)}), bf16[2,64,2,1280]{3,1,2,0:T(8,128)(2,1)S(1)}, u32[]{:S(2)}, u32[]{:S(2)}) async-start(bf16[2,64,2,1280]{3,1,2,0:T(8,128)(2,1)} %bitcast.14), calls=%async_computation | async-start | bytes 1310720 | tf_op jit(solution)/shard_map/all_to_all | solution.py:26
  33.4 4.4 %copy-start.4 = (f32[1280]{0:T(1024)S(1)}, f32[1280]{0:T(1024)}, u32[]{:S(2)}) copy-start(f32[1280]{0:T(1024)} %param.17) | copy-start | bytes 15364
  40.9 18.0 %copy-start.3 = (bf16[128,2048]{1,0:T(8,128)(2,1)S(1)}, bf16[128,2048]{1,0:T(8,128)(2,1)}, u32[]{:S(2)}) copy-start(bf16[128,2048]{1,0:T(8,128)(2,1)} %param.20) | copy-start | bytes 1572868
  44.4 56.1 %all-to-all-start.1 = ((bf16[2,64,2,2560]{3,2,0,1:T(2,128)(2,1)}), bf16[2,64,2,2560]{3,2,0,1:T(2,128)(2,1)S(1)}, u32[]{:S(2)}, u32[]{:S(2)}) async-start(bf16[2,64,2,2560]{3,2,0,1:T(2,128)(2,1)} %copy.109), calls=%async_computation.1 | async-start | bytes 2621440 | tf_op jit(solution)/shard_map/all_to_all | solution.py:115
  174.5 6.4 %copy-start.2 = (f32[2,1024,128]{2,1,0:T(8,128)S(1)}, f32[2,1024,128]{2,1,0:T(8,128)}, u32[]{:S(2)}) copy-start(f32[2,1024,128]{2,1,0:T(8,128)} %custom-call.2) | copy-start | bytes 3145732
Sparse Core Ops, SparseCore 0:
  11.4 150.7 all-gather.1
where the time goes:
time: 339 us; the launch traced here: 336 us
  waiting for transfers between devices  97.9 us (29%)
  matrix products  94.6 us (28%)
  local copies, waits for them, and re-layouts  64.3 us (19%)
  other arithmetic  29.7 us (9%)
  starting transfers between devices  20.2 us (6%)
  between operations  14.3 us (4%)
  loops' own time  10.4 us (3%)
  blocking collectives  4.79 us (1%)
    all_gather x1, waiting for transfers between devices, side_by_side(): result = lax.all_gather(both, axis, axis=dim, tiled=True)  54.7 us
    dot_general x16, matrix products, attend_block(): jnp.einsum('hrk,khd->hrd', weights.astype(jnp.bfloat16), value_block, pre...  52.4 us
    all_to_all x1, waiting for transfers between devices, deliver_tokens(): lax.all_to_all(outgoing.reshape(sections, owner_count // sections, capaci...  40.6 us
    dot_general x16, matrix products, attend_block(): jnp.einsum('hrd,khd->hrk', query_heads, key_block, preferred_element_type...  31.3 us
    split x3, local copies, waits for them, and re-layouts, side_by_side(): jnp.split(result, [sum(widths[:k]) for k in range(1, len(widths))], axis=...  18.7 us
    reduce_sum x16, other arithmetic, attend_block(): denominator = denominator * factor + jnp.sum(weights, axis=-1)  17.7 us
    all_to_all x1, starting transfers between devices, deliver_tokens(): lax.all_to_all(outgoing.reshape(sections, owner_count // sections, capaci...  14.5 us
    dynamic_slice x16, local copies, waits for them, and re-layouts, one_step(): key_docs = lax.dynamic_slice_in_dim(documents, block_start, block_size, 0)  12.2 us
  transfers between devices with their start and end apart: 3, of which 3 were waited for; matrix products, arithmetic and copies ran while one was open for 9% of the time, Pallas kernels for 0%

commit v1 on v0

v1 whole, which is shorter than its diff:
```python
import math

import jax
import jax.numpy as jnp
from jax import lax
from jax.experimental import pallas as pl
from jax.experimental.pallas import tpu as pltpu
from jax.sharding import PartitionSpec as P


HD = 128
EPSILON = 1e-06
BOTH = ("section", "seq")
BF = jnp.bfloat16
F32 = jnp.float32
NZ, NY, NX = 8, 2, 4
QUAD = 512
NT = (((1,), (1,)), ((), ()))


def vision_kernel(m_ref, x_ref, w_hbm, gain_ref, ow_hbm, win_ref, send_ref, keep_ref,
                  w_buf, ow_buf, ctx_ref, part_ref, xp_ref, sems):
    copies = [pltpu.make_async_copy(w_hbm.at[i], w_buf.at[i], sems.at[i]) for i in range(3)]
    copies.append(pltpu.make_async_copy(ow_hbm, ow_buf, sems.at[3]))
    for c in copies:
        c.start()
    rows = x_ref.shape[0]
    i = lax.broadcasted_iota(jnp.int32, (rows, rows), 0)
    j = lax.broadcasted_iota(jnp.int32, (rows, rows), 1)
    tokens = rows // 4
    perm = jnp.where(j == 4 * (i & (tokens - 1)) + i // tokens, 1.0, 0.0).astype(BF)
    xp = jnp.dot(perm, x_ref[...], preferred_element_type=F32)
    xp_ref[...] = xp
    scale = lax.rsqrt(jnp.mean(xp * xp, axis=-1, keepdims=True) + EPSILON)
    normed = (xp * scale * gain_ref[...]).astype(BF)
    win = jnp.broadcast_to(win_ref[...], (128, rows)).astype(F32).astype(BF)
    win_row = lax.dot_general(win, perm, NT, preferred_element_type=F32)[0:1]
    win_col = lax.dot_general(perm, win, NT, preferred_element_type=F32)[:, 0:1]
    allowed = win_row == win_col
    heads = []
    for n in range(3):
        copies[n].wait()
        heads.append(jnp.dot(normed, w_buf[n], preferred_element_type=F32).astype(BF))
    q, k, v = heads
    hd = 80
    local = q.shape[1] // hd
    for h in range(local):
        lo, hi = h * hd, (h + 1) * hd
        a, b = lo // 128 * 128, -(-hi // 128) * 128
        col = lax.broadcasted_iota(jnp.int32, (rows, b - a), 1) + a
        mine = (col >= lo) & (col < hi)
        qh = jnp.where(mine, q[:, a:b].astype(F32), 0.0).astype(BF)
        s = lax.dot_general(qh, k[:, a:b], NT, preferred_element_type=F32) * (1.0 / math.sqrt(hd))
        s = jnp.where(allowed, s, -1e30)
        p = jnp.exp(s - jnp.max(s, axis=-1, keepdims=True))
        den = jnp.sum(p, axis=-1, keepdims=True)
        o = jnp.dot(p.astype(BF), v[:, a:b], preferred_element_type=F32) / den
        if lo == a:
            ctx_ref[:, a:b] = o
        else:
            ctx_ref[:, a:b] = jnp.where(mine, o, ctx_ref[:, a:b] if b - a == 128 else
                                        jnp.concatenate([ctx_ref[:, a:a + 128], o[:, 128:]], axis=1))
    copies[3].wait()
    part_ref[...] = jnp.dot(ctx_ref[...].astype(BF), ow_buf[...], preferred_element_type=F32)
    half = rows // 2
    m = m_ref[0]
    own = pl.multiple_of(m * half, half)
    other = pl.multiple_of((1 - m) * half, half)
    send_ref[...] = part_ref[pl.ds(other, half), :].astype(BF)
    keep_ref[...] = part_ref[pl.ds(own, half), :] + xp_ref[pl.ds(own, half), :]


def vision(m, patches, inner_weight, norm_gain, outer_weight, windows):
    rows, vd = patches.shape
    cols = inner_weight.shape[2]
    vm = pl.BlockSpec(memory_space=pltpu.VMEM)
    hbm = pl.BlockSpec(memory_space=pl.ANY)
    return pl.pallas_call(
        vision_kernel,
        in_specs=[pl.BlockSpec(memory_space=pltpu.SMEM), vm, hbm, vm, hbm, vm],
        out_specs=[vm, vm],
        out_shape=[jax.ShapeDtypeStruct((rows // 2, vd), BF), jax.ShapeDtypeStruct((rows // 2, vd), F32)],
        scratch_shapes=[
            pltpu.VMEM((3, vd, cols), BF),
            pltpu.VMEM((cols, vd), BF),
            pltpu.VMEM((rows, cols), F32),
            pltpu.VMEM((rows, vd), F32),
            pltpu.VMEM((rows, vd), F32),
            pltpu.SemaphoreType.DMA((4,)),
        ],
        cost_estimate=pl.CostEstimate(flops=3 * 10**9, bytes_accessed=8 * 10**6, transcendentals=10**6),
        name="vision",
    )(m, patches, inner_weight, norm_gain.reshape(1, vd), outer_weight, windows)


def merge_kernel(keep_ref, recv_ref, gain_ref, target_ref, out_ref):
    r = keep_ref[...] + recv_ref[...].astype(F32)
    merged = (r * lax.rsqrt(jnp.mean(r * r, axis=-1, keepdims=True) + EPSILON) * gain_ref[...]).astype(BF)
    half = r.shape[0] // 2
    w = r.shape[1] // 2
    quarters = jnp.concatenate(
        [merged[:half, :w], merged[:half, w:], merged[half:, :w], merged[half:, w:]], axis=0)
    n = out_ref.shape[0]
    step = 256
    for b in range(n // step):
        i = lax.broadcasted_iota(jnp.int32, (step, 4 * half), 0) + b * step
        place = jnp.where(target_ref[...] == i, 1.0, 0.0).astype(BF)
        out_ref[b * step:(b + 1) * step, :] = jnp.dot(
            place, quarters, preferred_element_type=F32).astype(BF)


def merge(keep, recv, merge_gain, target, slots):
    vm = pl.BlockSpec(memory_space=pltpu.VMEM)
    return pl.pallas_call(
        merge_kernel,
        in_specs=[vm] * 4,
        out_specs=vm,
        out_shape=jax.ShapeDtypeStruct((slots * 4, keep.shape[1] // 2), BF),
        cost_estimate=pl.CostEstimate(flops=4 * 10**8, bytes_accessed=3 * 10**6, transcendentals=10**4),
        name="merge",
    )(keep, recv, merge_gain.reshape(1, -1), target)


def place_kernel(in_ref, out_ref):
    n, w = in_ref.shape
    i = lax.broadcasted_iota(jnp.int32, (n, n), 0)
    j = lax.broadcasted_iota(jnp.int32, (n, n), 1)
    quarter = n // 4
    perm = jnp.where(j == 4 * (i & (quarter - 1)) + i // quarter, 1.0, 0.0).astype(BF)
    y = jnp.dot(perm, in_ref[...], preferred_element_type=F32).astype(BF)
    for q in range(4):
        out_ref[:, q * w:(q + 1) * w] = y[q * quarter:(q + 1) * quarter]


def place(arrived):
    n, w = arrived.shape
    step = 256
    return pl.pallas_call(
        place_kernel,
        grid=(n // step,),
        in_specs=[pl.BlockSpec((step, w), lambda i: (i, 0))],
        out_specs=pl.BlockSpec((step // 4, 4 * w), lambda i: (i, 0)),
        out_shape=jax.ShapeDtypeStruct((n // 4, 4 * w), BF),
        cost_estimate=pl.CostEstimate(flops=4 * 10**8, bytes_accessed=3 * 10**6, transcendentals=0),
        name="place",
    )(arrived)


def perm_of(move):
    pairs = []
    for c in range(2):
        for z in range(NZ):
            for y in range(NY):
                for x in range(NX):
                    a, b, d, e = move(c, z, y, x)
                    pairs.append((((c * NZ + z) * NY + y) * NX + x, ((a * NZ + b) * NY + d) * NX + e))
    return pairs


def quad_move(p):
    return perm_of(lambda c, z, y, x: (z >> 1 & 1, 2 * (2 * c + (p ^ z >> 2)) + (z & 1), y, x))


def attend_kernel(meta_ref, q_ref, *rest):
    near, far = rest[:4], rest[4:8]
    starts_ref, ends_ref, o_ref, q_scr, m_scr, acc_scr = rest[8:]
    x, c, here, first = [meta_ref[n] for n in range(4)]
    chips = [x, (x + 3) & 3, (x + 1) & 3, (x + 2) & 3]
    starts, ends = starts_ref[...], ends_ref[...]
    chain = q_scr.shape[0] // 2

    def same_doc(base, n):
        at = lax.broadcasted_iota(jnp.int32, (n, HD), 0) + base
        return (at >= starts) & (at < ends)

    other = jnp.where(same_doc(here * QUAD + x * 128, 128), 0.0, -1e30).astype(BF)
    for g in range(8):
        q_scr[g * 128:(g + 1) * 128, :HD] = other
        q_scr[g * 128:(g + 1) * 128, HD:] = q_ref[:, g * 128:(g + 1) * 128]
    factor = math.log2(math.e) / math.sqrt(HD)

    def keys_of(b):
        at, hi = (b ^ here) & 3, b >> 3
        own = (b >> 2 & 1) == c
        kv = jnp.concatenate(
            [jnp.where(own, n[at, hi], f[at, hi]) for n, f in zip(near, far)], axis=0)
        same = jnp.concatenate(
            [jnp.where(same_doc(b * QUAD + t * 128, 128), 1.0, 0.0) for t in chips], axis=0).astype(BF)
        return (jnp.concatenate([same, kv[:, :HD]], axis=1),
                jnp.concatenate([kv[:, HD:], jnp.ones((QUAD, HD), BF)], axis=1))

    i = lax.broadcasted_iota(jnp.int32, (chain, QUAD), 0)
    j = lax.broadcasted_iota(jnp.int32, (chain, QUAD), 1)
    ahead = jnp.where(j < 128, x, jnp.where(j < 256, chips[1], jnp.where(j < 384, chips[2], chips[3])))
    causal = ahead * 128 + (j & 127) <= x * 128 + (i & 127)
    keys, values = keys_of(here)
    for g in range(2):
        part = pl.ds(g * chain, chain)
        s = lax.dot_general(q_scr[part], keys, NT, preferred_element_type=F32)
        s = jnp.where(causal, s, -1e30)
        new = jnp.broadcast_to(jnp.max(s, axis=-1, keepdims=True), (chain, HD))
        m_scr[part] = new
        w = jnp.exp2((s - jnp.tile(new, (1, QUAD // HD))) * factor)
        acc_scr[part] = jnp.dot(w.astype(BF), values, preferred_element_type=F32)

    @pl.loop(first, here)
    def _(b):
        keys, values = keys_of(b)
        for g in range(2):
            part = pl.ds(g * chain, chain)
            s = lax.dot_general(q_scr[part], keys, NT, preferred_element_type=F32)
            old = m_scr[part]
            new = jnp.maximum(old, jnp.max(s, axis=-1, keepdims=True))
            m_scr[part] = new
            w = jnp.exp2((s - jnp.tile(new, (1, QUAD // HD))) * factor)
            alpha = jnp.exp2((old - new) * factor)
            acc_scr[part] = acc_scr[part] * jnp.tile(alpha, (1, 2)) + jnp.dot(
                w.astype(BF), values, preferred_element_type=F32)

    for g in range(8):
        part = pl.ds(g * 128, 128)
        o_ref[:, g * 128:(g + 1) * 128] = (acc_scr[part, :HD] / acc_scr[part, HD:]).astype(BF)


def attend(meta, query, near, far, starts, ends):
    pieces = [*near, *far]
    vm = pl.BlockSpec(memory_space=pltpu.VMEM)
    return pl.pallas_call(
        attend_kernel,
        in_specs=[pl.BlockSpec(memory_space=pltpu.SMEM)] + [vm] * 11,
        out_specs=vm,
        out_shape=jax.ShapeDtypeStruct((128, 1024), BF),
        scratch_shapes=[
            pltpu.VMEM((1024, 2 * HD), BF),
            pltpu.VMEM((1024, HD), F32),
            pltpu.VMEM((1024, 2 * HD), F32),
        ],
        compiler_params=pltpu.CompilerParams(vmem_limit_bytes=32 << 20),
        cost_estimate=pl.CostEstimate(flops=4 * 10**9, bytes_accessed=3 * 10**6, transcendentals=5 * 10**6),
        name="attend",
    )(meta, query, *pieces, starts, ends)


def pack_kernel(*refs):
    for n, ref in enumerate(refs[:-1]):
        refs[-1][n] = ref[...]


def pack(parts):
    vm = pl.BlockSpec(memory_space=pltpu.VMEM)
    return pl.pallas_call(
        pack_kernel,
        in_specs=[vm] * len(parts),
        out_specs=vm,
        out_shape=jax.ShapeDtypeStruct((len(parts),) + parts[0].shape, BF),
        cost_estimate=pl.CostEstimate(flops=0, bytes_accessed=10**6, transcendentals=0),
        name="pack",
    )(*parts)


def context_part(context_query, context_key, context_value, documents):
    c = lax.axis_index("section")
    s = lax.axis_index("seq")
    z, y, x = s // (NX * NY), (s // NX) % NY, s % NX
    a, par = z // 2, z & 1
    odd, hi = a & 1, a >> 1
    head = [
        jnp.concatenate([t[:, j * HD:(j + 1) * HD] for t in (context_key, context_value)], axis=1)
        for j in range(2)
    ]
    got = []
    for p in range(2):
        got.append(lax.ppermute(jnp.where((hi ^ p) == 0, head[0], head[1]), BOTH, quad_move(p)))
    mine = jnp.where(odd == 0, jnp.stack(got), jnp.stack(got[::-1]))
    parts = [mine]
    for d, e in ((0, 1), (1, 0), (1, 1)):
        parts.append(lax.ppermute(mine, "seq", [(t, t ^ (8 * d + 4 * e)) for t in range(64)]))
    near = [pack(parts)]
    for step in (1, -1, 2):
        near.append(lax.ppermute(near[0], "seq", [(t, t // 4 * 4 + (t + step) % 4) for t in range(64)]))
    far = []
    for n in range(4):
        far.append(lax.ppermute(near[n], "section", [(0, 1), (1, 0)]))
    queries = []
    for p in range(2):
        queries.append(lax.ppermute(
            jnp.where((hi ^ p) == 0, context_query[:, :1024], context_query[:, 1024:]),
            BOTH, quad_move(p)))
    place = [(2 * (p ^ odd) + c) * 2048 + (s & 15) * 128 for p in range(2)]
    row_docs = jnp.stack([lax.dynamic_slice_in_dim(documents, t, 1, 0)[0] for t in place])
    firsts = jnp.sum(documents[None, :] < row_docs[:, None], axis=1).astype(jnp.int32) // QUAD
    names = jnp.arange(8, dtype=jnp.int32)
    pad = jnp.full((HD - 8,), 8192, jnp.int32)
    starts = jnp.sum(documents[None, :] < names[:, None], axis=1).astype(jnp.int32)
    ends = jnp.sum(documents[None, :] <= names[:, None], axis=1).astype(jnp.int32)
    starts = jnp.concatenate([starts, pad]).reshape(1, HD)
    ends = jnp.concatenate([ends, pad]).reshape(1, HD)
    back = []
    for p in range(2):
        meta = jnp.stack([x, c, (2 * (p ^ odd) + c) * 4 + par * 2 + y, firsts[p]]).astype(jnp.int32)
        o = attend(meta, queries[p], near, far, starts, ends)
        back.append(lax.ppermute(o, BOTH, [(t, f) for f, t in quad_move(p)]))
    return jnp.where(hi == 0, jnp.concatenate(back, axis=1), jnp.concatenate(back[::-1], axis=1))


def program(
    patches,
    inner_weight,
    norm_gain,
    outer_weight,
    merge_gain,
    windows,
    owners,
    context_query,
    context_key,
    context_value,
    documents,
):
    m = lax.axis_index("mp").astype(jnp.int32).reshape(1)
    send, keep = vision(m, patches, inner_weight, norm_gain, outer_weight, windows)
    recv = lax.ppermute(send, "mp", [(0, 1), (1, 0)])
    tokens = owners.shape[0]
    target = owners[:, 0]
    order = jnp.arange(tokens, dtype=jnp.int32)
    earlier = (target[:, None] == target[None, :]) & (order[:, None] < order[None, :])
    slot = target * 2 + jnp.sum(earlier, axis=0).astype(jnp.int32)
    spot = (4 * slot[None, :] + jnp.arange(4, dtype=jnp.int32)[:, None]).reshape(1, 4 * tokens)
    owner_count = lax.axis_size(BOTH)
    outgoing = merge(keep, recv, merge_gain, spot, owner_count * 2)
    arrived = lax.all_to_all(
        outgoing.reshape(owner_count, 8, outgoing.shape[1]), BOTH, split_axis=0, concat_axis=0, tiled=True)
    delivered = place(arrived.reshape(outgoing.shape))
    attended = context_part(context_query, context_key, context_value, documents)
    return (delivered, attended)


def solution(mesh):
    in_specs = (
        P(BOTH, None),
        P(None, None, "mp"),
        P(),
        P("mp", None),
        P(),
        P(BOTH, None),
        P(BOTH, None),
        P("seq", ("section", "mp")),
        P("seq", ("section", "mp")),
        P("seq", ("section", "mp")),
        P(),
    )
    out_specs = (P(BOTH, "mp"), P("seq", ("section", "mp")))
    return jax.shard_map(program, mesh=mesh, in_specs=in_specs, out_specs=out_specs, check_vma=False)
```

time: 339 us -> 138 us (0.41)
  the two profiles are of different devices: /device:TPU:8 before, /device:TPU:113 now
where the time goes in v1:
time: 138 us; the launch traced here: 137 us
  starting transfers between devices  52 us (38%)
  waiting for transfers between devices  43.8 us (32%)
  Pallas kernels  26.3 us (19%)
  local copies, waits for them, and re-layouts  8.89 us (6%)
  other arithmetic  5.36 us (4%)
    ppermute x3, waiting for transfers between devices, context_part(): lax.ppermute(near[0], 'seq', [(t, t // 4 * 4 + (t + step) % 4) for t in r...  24 us
    all_to_all x1, starting transfers between devices, program(): lax.all_to_all(outgoing.reshape(owner_count, 8, outgoing.shape[1]), BOTH,...  15.6 us
    ppermute x2, waiting for transfers between devices, context_part(): back.append(lax.ppermute(o, BOTH, [(t, f) for f, t in quad_move(p)]))  14.7 us
    ppermute x2, starting transfers between devices, context_part(): back.append(lax.ppermute(o, BOTH, [(t, f) for f, t in quad_move(p)]))  12.4 us
    pallas_call x2, Pallas kernels, attend(): pl.pallas_call(attend_kernel, in_specs=[pl.BlockSpec(memory_space=pltpu.S...  10.1 us
    pallas_call x1, Pallas kernels, vision(): pl.pallas_call(vision_kernel, in_specs=[pl.BlockSpec(memory_space=pltpu.S...  7.3 us
    ppermute x2, starting transfers between devices, context_part(): lax.ppermute(jnp.where(hi ^ p == 0, context_query[:, :1024], context_quer...  7.01 us
    ppermute x2, starting transfers between devices, context_part(): lax.ppermute(jnp.where(hi ^ p == 0, head[0], head[1]), BOTH, quad_move(p))  5.3 us
  transfers between devices with their start and end apart: 18, of which 5 were waited for; matrix products, arithmetic and copies ran while one was open for 7% of the time, Pallas kernels for 16%

profile of v1, /device:TPU:113, one launch (start us, length us, event | category | flops | bytes accessed | tf_op | source)
XLA Modules:
  0.0 137.3 jit_solution(7087357366258451482)
XLA Ops:
  0.7 0.8 fusion.2
  1.5 5.2 %collective-permute-start.2 = (bf16[128,256]{1,0:T(8,128)(2,1)S(1)}, bf16[128,256]{1,0:T(8,128)(2,1)S(1)}, u32[]{:S(2)}, u32[]{:S(2)}) collective-permute-start(bf16[128,256]{1,0:T(8,128)(2,1)S(1)} %get-tuple-element.10), channel_id=1, source_target_pairs={{0,0},{2,2},{4,4},{6,6},{8,8},{10,10},{12,12},{14,14},{16,16},{18,... | collective-permute-start | bytes 196616 | tf_op jit(solution)/shard_map/ppermute | solution.py:273
  6.9 1.3 reshape.62.gain_ref
  8.2 7.3 %vision.1 = (bf16[128,1280]{1,0:T(8,128)(2,1)}, f32[128,1280]{1,0:T(8,128)}) custom-call(s32[1]{0:T(128)} %bitcast.m_ref, bf16[256,1280]{1,0:T(8,128)(2,1)} %x_ref.1, bf16[3,1280,640]{2,1,0:T(8,128)(2,1)} %w_hbm.1, f32[1,1280]{1,0:T(1,128)} %reshape.62.gain_ref, bf16[640,1280]{1,0:T(8,128)(2,1)} %ow_hbm.1, s32[1,256]{1,0:T(1,128)} %win_ref.1), custom_call_target="tpu_custom_call" | custom-call | flops 3000000000 | bytes 8000000 | tf_op jit(solution)/shard_map/vision/pallas_call | solution.py:78
  15.5 1.1 collective-permute-start
  17.2 0.7 collective-permute-start.5
  17.9 3.1 %collective-permute-start.6 = (bf16[2,128,256]{2,1,0:T(8,128)(2,1)S(1)}, bf16[2,128,256]{2,1,0:T(8,128)(2,1)S(1)}, u32[]{:S(2)}, u32[]{:S(2)}) collective-permute-start(bf16[2,128,256]{2,1,0:T(8,128)(2,1)S(1)} %maximum_select_fusion.1.refs_0_), channel_id=1, source_target_pairs={{0,24},{2,26},{4,28},{6,30},{8,16},{10,18},{12,20},{14,22},{16,8},... | collective-permute-start | bytes 393224 | tf_op jit(solution)/shard_map/ppermute | solution.py:277
  22.2 5.1 %collective-permute-done.recv_ref = bf16[128,1280]{1,0:T(8,128)(2,1)S(1)} collective-permute-done((bf16[128,1280]{1,0:T(8,128)(2,1)}, bf16[128,1280]{1,0:T(8,128)(2,1)S(1)}, u32[]{:S(2)}, u32[]{:S(2)}) %collective-permute-start) | collective-permute-done | bytes 327712 | tf_op jit(solution)/shard_map/ppermute | solution.py:321
  28.1 3.0 %merge.1 = bf16[1024,640]{1,0:T(8,128)(2,1)} custom-call(f32[128,1280]{1,0:T(8,128)} %get-tuple-element.4.keep_ref, bf16[128,1280]{1,0:T(8,128)(2,1)} %copy-done.4, f32[1,1280]{1,0:T(1,128)} %reshape.63.gain_ref, s32[1,256]{1,0:T(1,128)} %add.81.target_ref), custom_call_target="tpu_custom_call" | custom-call | flops 400000000 | bytes 3000000 | tf_op jit(solution)/shard_map/merge/pallas_call | solution.py:114
  31.1 15.6 %all-to-all-start = ((bf16[128,8,640]{2,1,0:T(8,128)(2,1)}), bf16[128,8,640]{2,1,0:T(8,128)(2,1)S(1)}, u32[]{:S(2)}, u32[]{:S(2)}) async-start(bf16[128,8,640]{2,1,0:T(8,128)(2,1)} %bitcast.16), calls=%async_computation | async-start | bytes 2621440 | tf_op jit(solution)/shard_map/all_to_all | solution.py:330
  48.0 1.9 %pack.1.rest_0_ = bf16[4,2,128,256]{3,2,1,0:T(8,128)(2,1)} custom-call(bf16[2,128,256]{2,1,0:T(8,128)(2,1)} %copy-done.3, bf16[2,128,256]{2,1,0:T(8,128)(2,1)} %copy-done.6, bf16[2,128,256]{2,1,0:T(8,128)(2,1)} %copy-done.7, bf16[2,128,256]{2,1,0:T(8,128)(2,1)} %copy-done.8), custom_call_target="tpu_custom_call" | custom-call | bytes 1000000 | tf_op jit(solution)/shard_map/pack/pallas_call | solution.py:251
  50.0 1.2 collective-permute-start.7
  51.1 1.5 %collective-permute-start.8 = (bf16[4,2,128,256]{3,2,1,0:T(8,128)(2,1)}, bf16[4,2,128,256]{3,2,1,0:T(8,128)(2,1)S(1)}, u32[]{:S(2)}, u32[]{:S(2)}) collective-permute-start(bf16[4,2,128,256]{3,2,1,0:T(8,128)(2,1)} %pack.1.rest_0_), channel_id=1, source_target_pairs={{0,6},{2,0},{4,2},{6,4},{8,14},{10,8},{12,10},{14,12},{16,22},{18,... | collective-permute-start | bytes 1572872 | tf_op jit(solution)/shard_map/ppermute | solution.py:280
  52.6 1.5 %collective-permute-start.9 = (bf16[4,2,128,256]{3,2,1,0:T(8,128)(2,1)}, bf16[4,2,128,256]{3,2,1,0:T(8,128)(2,1)S(1)}, u32[]{:S(2)}, u32[]{:S(2)}) collective-permute-start(bf16[4,2,128,256]{3,2,1,0:T(8,128)(2,1)} %pack.1.rest_0_), channel_id=1, source_target_pairs={{0,4},{2,6},{4,0},{6,2},{8,12},{10,14},{12,8},{14,10},{16,20},{18,... | collective-permute-start | bytes 1572872 | tf_op jit(solution)/shard_map/ppermute | solution.py:280
  54.1 0.8 broadcast_select_fusion.1
  55.0 4.6 %collective-permute-start.1 = (bf16[128,1024]{1,0:T(8,128)(2,1)}, bf16[128,1024]{1,0:T(8,128)(2,1)S(1)}, u32[]{:S(2)}, u32[]{:S(2)}) collective-permute-start(bf16[128,1024]{1,0:T(8,128)(2,1)} %get-tuple-element.8), channel_id=1, source_target_pairs={{0,0},{2,2},{4,4},{6,6},{8,8},{10,10},{12,12},{14,14},{16,16},{18,... | collective-permute-start | bytes 786440 | tf_op jit(solution)/shard_map/ppermute | solution.py:286
  60.3 1.5 %pad_add_fusion = s32[2]{0:T(128)S(1)} fusion(s32[1]{0:T(128)} %get-tuple-element.17, s32[1]{0:T(128)} %get-tuple-element.16), kind=kLoop, calls=%fused_computation.22 | loop fusion | flops 2 | bytes 16 | tf_op jit(solution)/shard_map/stack | solution.py:290
  62.1 11.3 %collective-permute-done.7.rest_1_ = bf16[4,2,128,256]{3,2,1,0:T(8,128)(2,1)S(1)} collective-permute-done((bf16[4,2,128,256]{3,2,1,0:T(8,128)(2,1)}, bf16[4,2,128,256]{3,2,1,0:T(8,128)(2,1)S(1)}, u32[]{:S(2)}, u32[]{:S(2)}) %collective-permute-start.7) | collective-permute-done | bytes 524320 | tf_op jit(solution)/shard_map/ppermute | solution.py:280
  73.4 0.8 collective-permute-start.11
  74.9 12.7 %collective-permute-done.9.rest_3_ = bf16[4,2,128,256]{3,2,1,0:T(8,128)(2,1)S(1)} collective-permute-done((bf16[4,2,128,256]{3,2,1,0:T(8,128)(2,1)}, bf16[4,2,128,256]{3,2,1,0:T(8,128)(2,1)S(1)}, u32[]{:S(2)}, u32[]{:S(2)}) %collective-permute-start.9) | collective-permute-done | bytes 524320 | tf_op jit(solution)/shard_map/ppermute | solution.py:280
  88.9 0.8 pad_add_fusion.1.meta_ref
  89.6 0.8 pad_add_fusion.3.meta_ref
  90.6 2.4 %collective-permute-start.15 = (bf16[128,1024]{1,0:T(8,128)(2,1)}, bf16[128,1024]{1,0:T(8,128)(2,1)S(1)}, u32[]{:S(2)}, u32[]{:S(2)}) collective-permute-start(bf16[128,1024]{1,0:T(8,128)(2,1)} %get-tuple-element.9), channel_id=1, source_target_pairs={{0,32},{2,34},{4,36},{6,38},{8,40},{10,42},{12,44},{14,46},{16,48}... | collective-permute-start | bytes 786440 | tf_op jit(solution)/shard_map/ppermute | solution.py:286
  93.1 1.0 copy-done
  94.1 2.9 %attend.2 = bf16[128,1024]{1,0:T(8,128)(2,1)S(1)} custom-call(s32[4]{0:T(128)S(1)} %pad_add_fusion.1.meta_ref, bf16[128,1024]{1,0:T(8,128)(2,1)S(1)} %collective-permute-done.1.q_ref, bf16[4,2,128,256]{3,2,1,0:T(8,128)(2,1)S(1)} %copy-done, bf16[4,2,128,256]{3,2,1,0:T(8,128)(2,1)S(1)} %collective-permute-done.7.rest_1_, ...), custom_call_target="tpu_custom_call" | custom-call | flops 4000000000 | bytes 3000000 | tf_op jit(solution)/shard_map/attend/pallas_call | solution.py:228
  97.0 12.3 %collective-permute-start.14 = (bf16[128,1024]{1,0:T(8,128)(2,1)S(1)}, bf16[128,1024]{1,0:T(8,128)(2,1)S(1)}, u32[]{:S(2)}, u32[]{:S(2)}) collective-permute-start(bf16[128,1024]{1,0:T(8,128)(2,1)S(1)} %attend.2), channel_id=1, source_target_pairs={{0,0},{2,2},{4,4},{6,6},{8,8},{10,10},{12,12},{14,14},{16,16},{18,... | collective-permute-start | bytes 786440 | tf_op jit(solution)/shard_map/ppermute | solution.py:302
  109.3 7.2 %attend.3 = bf16[128,1024]{1,0:T(8,128)(2,1)S(1)} custom-call(s32[4]{0:T(128)S(1)} %pad_add_fusion.3.meta_ref, bf16[128,1024]{1,0:T(8,128)(2,1)S(1)} %collective-permute-done.15.q_ref, bf16[4,2,128,256]{3,2,1,0:T(8,128)(2,1)S(1)} %copy-done, bf16[4,2,128,256]{3,2,1,0:T(8,128)(2,1)S(1)} %collective-permute-done.7.rest_1_, ...), custom_call_target="tpu_custom_call" | custom-call | flops 4000000000 | bytes 3000000 | tf_op jit(solution)/shard_map/attend/pallas_call | solution.py:228
  116.6 3.3 %collective-permute-done.14 = bf16[128,1024]{1,0:T(8,128)(2,1)S(1)} collective-permute-done((bf16[128,1024]{1,0:T(8,128)(2,1)S(1)}, bf16[128,1024]{1,0:T(8,128)(2,1)S(1)}, u32[]{:S(2)}, u32[]{:S(2)}) %collective-permute-start.14) | collective-permute-done | bytes 262176 | tf_op jit(solution)/shard_map/ppermute | solution.py:302
  119.9 11.4 %collective-permute-done.16 = bf16[128,1024]{1,0:T(8,128)(2,1)S(1)} collective-permute-done((bf16[128,1024]{1,0:T(8,128)(2,1)S(1)}, bf16[128,1024]{1,0:T(8,128)(2,1)S(1)}, u32[]{:S(2)}, u32[]{:S(2)}) %collective-permute-start.16) | collective-permute-done | bytes 262176 | tf_op jit(solution)/shard_map/ppermute | solution.py:302
  131.3 0.9 maximum_select_fusion
  132.3 1.1 copy-done.1
  133.3 4.0 %place.1 = bf16[256,2560]{1,0:T(8,128)(2,1)} custom-call(bf16[1024,640]{1,0:T(8,128)(2,1)} %bitcast.15), custom_call_target="tpu_custom_call" | custom-call | flops 400000000 | bytes 3000000 | tf_op jit(solution)/shard_map/place/pallas_call | solution.py:138
  (52 shorter events, 7.4 us)
Async XLA Ops:
  1.5 15.1 %collective-permute-start.2 = (bf16[128,256]{1,0:T(8,128)(2,1)S(1)}, bf16[128,256]{1,0:T(8,128)(2,1)S(1)}, u32[]{:S(2)}, u32[]{:S(2)}) collective-permute-start(bf16[128,256]{1,0:T(8,128)(2,1)S(1)} %get-tuple-element.10), channel_id=1, source_target_pairs={{0,0},{2,2},{4,4},{6,6},{8,8},{10,10},{12,12},{14,14},{16,16},{18,... | collective-permute-start | bytes 196616 | tf_op jit(solution)/shard_map/ppermute | solution.py:273
  6.8 9.9 %collective-permute-start.3 = (bf16[128,256]{1,0:T(8,128)(2,1)S(1)}, bf16[128,256]{1,0:T(8,128)(2,1)S(1)}, u32[]{:S(2)}, u32[]{:S(2)}) collective-permute-start(bf16[128,256]{1,0:T(8,128)(2,1)S(1)} %get-tuple-element.11), channel_id=1, source_target_pairs={{0,32},{2,34},{4,36},{6,38},{8,40},{10,42},{12,44},{14,46},{16,48}... | collective-permute-start | bytes 196616 | tf_op jit(solution)/shard_map/ppermute | solution.py:273
  8.2 8.4 %copy-start.10 = (s32[64,1]{0,1:T(1,128)S(1)}, s32[64,1]{0,1:T(1,128)}, u32[]{:S(2)}) copy-start(s32[64,1]{0,1:T(1,128)} %param.17) | copy-start | bytes 772
  8.2 12.8 %copy-start.9 = (f32[1280]{0:T(1024)S(1)}, f32[1280]{0:T(1024)}, u32[]{:S(2)}) copy-start(f32[1280]{0:T(1024)} %param.15) | copy-start | bytes 15364
  15.5 11.9 %collective-permute-start = (bf16[128,1280]{1,0:T(8,128)(2,1)}, bf16[128,1280]{1,0:T(8,128)(2,1)S(1)}, u32[]{:S(2)}, u32[]{:S(2)}) collective-permute-start(bf16[128,1280]{1,0:T(8,128)(2,1)} %get-tuple-element.5), channel_id=1, source_target_pairs={{0,1},{1,0},{2,3},{3,2},{4,5},{5,4},{6,7},{7,6},{8,9},{9,8},{10,11... | collective-permute-start | bytes 983048 | tf_op jit(solution)/shard_map/ppermute | solution.py:321
  16.7 14.4 %copy-start.3 = (bf16[2,128,256]{2,1,0:T(8,128)(2,1)}, bf16[2,128,256]{2,1,0:T(8,128)(2,1)S(1)}, u32[]{:S(2)}) copy-start(bf16[2,128,256]{2,1,0:T(8,128)(2,1)S(1)} %maximum_select_fusion.1.refs_0_) | copy-start | bytes 393220
  16.7 30.0 %collective-permute-start.4 = (bf16[2,128,256]{2,1,0:T(8,128)(2,1)S(1)}, bf16[2,128,256]{2,1,0:T(8,128)(2,1)S(1)}, u32[]{:S(2)}, u32[]{:S(2)}) collective-permute-start(bf16[2,128,256]{2,1,0:T(8,128)(2,1)S(1)} %maximum_select_fusion.1.refs_0_), channel_id=1, source_target_pairs={{0,8},{2,10},{4,12},{6,14},{8,0},{10,2},{12,4},{14,6},{16,24},{18,... | collective-permute-start | bytes 393224 | tf_op jit(solution)/shard_map/ppermute | solution.py:277
  17.2 29.5 %collective-permute-start.5 = (bf16[2,128,256]{2,1,0:T(8,128)(2,1)S(1)}, bf16[2,128,256]{2,1,0:T(8,128)(2,1)S(1)}, u32[]{:S(2)}, u32[]{:S(2)}) collective-permute-start(bf16[2,128,256]{2,1,0:T(8,128)(2,1)S(1)} %maximum_select_fusion.1.refs_0_), channel_id=1, source_target_pairs={{0,16},{2,18},{4,20},{6,22},{8,24},{10,26},{12,28},{14,30},{16,0},... | collective-permute-start | bytes 393224 | tf_op jit(solution)/shard_map/ppermute | solution.py:277
  17.9 28.8 %collective-permute-start.6 = (bf16[2,128,256]{2,1,0:T(8,128)(2,1)S(1)}, bf16[2,128,256]{2,1,0:T(8,128)(2,1)S(1)}, u32[]{:S(2)}, u32[]{:S(2)}) collective-permute-start(bf16[2,128,256]{2,1,0:T(8,128)(2,1)S(1)} %maximum_select_fusion.1.refs_0_), channel_id=1, source_target_pairs={{0,24},{2,26},{4,28},{6,30},{8,16},{10,18},{12,20},{14,22},{16,8},... | collective-permute-start | bytes 393224 | tf_op jit(solution)/shard_map/ppermute | solution.py:277
  27.3 0.7 copy-start.4
  31.1 23.1 %copy-start.2 = (bf16[128,2048]{1,0:T(8,128)(2,1)S(1)}, bf16[128,2048]{1,0:T(8,128)(2,1)}, u32[]{:S(2)}) copy-start(bf16[128,2048]{1,0:T(8,128)(2,1)} %param.18) | copy-start | bytes 1572868
  31.1 101.2 %all-to-all-start = ((bf16[128,8,640]{2,1,0:T(8,128)(2,1)}), bf16[128,8,640]{2,1,0:T(8,128)(2,1)S(1)}, u32[]{:S(2)}, u32[]{:S(2)}) async-start(bf16[128,8,640]{2,1,0:T(8,128)(2,1)} %bitcast.16), calls=%async_computation | async-start | bytes 2621440 | tf_op jit(solution)/shard_map/all_to_all | solution.py:330
  46.7 12.9 %copy-start.5 = (s32[8192]{0:T(1024)S(1)}, s32[8192]{0:T(1024)}, u32[]{:S(2)}) copy-start(s32[8192]{0:T(1024)} %param.21) | copy-start | bytes 98308
  46.7 0.7 copy-start.6
  46.7 0.7 copy-start.7
  47.4 0.6 copy-start.8
  50.0 23.5 %collective-permute-start.7 = (bf16[4,2,128,256]{3,2,1,0:T(8,128)(2,1)}, bf16[4,2,128,256]{3,2,1,0:T(8,128)(2,1)S(1)}, u32[]{:S(2)}, u32[]{:S(2)}) collective-permute-start(bf16[4,2,128,256]{3,2,1,0:T(8,128)(2,1)} %pack.1.rest_0_), channel_id=1, source_target_pairs={{0,2},{2,4},{4,6},{6,0},{8,10},{10,12},{12,14},{14,8},{16,18},{18,... | collective-permute-start | bytes 1572872 | tf_op jit(solution)/shard_map/ppermute | solution.py:280
  51.1 23.0 %collective-permute-start.8 = (bf16[4,2,128,256]{3,2,1,0:T(8,128)(2,1)}, bf16[4,2,128,256]{3,2,1,0:T(8,128)(2,1)S(1)}, u32[]{:S(2)}, u32[]{:S(2)}) collective-permute-start(bf16[4,2,128,256]{3,2,1,0:T(8,128)(2,1)} %pack.1.rest_0_), channel_id=1, source_target_pairs={{0,6},{2,0},{4,2},{6,4},{8,14},{10,8},{12,10},{14,12},{16,22},{18,... | collective-permute-start | bytes 1572872 | tf_op jit(solution)/shard_map/ppermute | solution.py:280
  52.6 34.9 %collective-permute-start.9 = (bf16[4,2,128,256]{3,2,1,0:T(8,128)(2,1)}, bf16[4,2,128,256]{3,2,1,0:T(8,128)(2,1)S(1)}, u32[]{:S(2)}, u32[]{:S(2)}) collective-permute-start(bf16[4,2,128,256]{3,2,1,0:T(8,128)(2,1)} %pack.1.rest_0_), channel_id=1, source_target_pairs={{0,4},{2,6},{4,0},{6,2},{8,12},{10,14},{12,8},{14,10},{16,20},{18,... | collective-permute-start | bytes 1572872 | tf_op jit(solution)/shard_map/ppermute | solution.py:280
  55.0 35.7 %collective-permute-start.1 = (bf16[128,1024]{1,0:T(8,128)(2,1)}, bf16[128,1024]{1,0:T(8,128)(2,1)S(1)}, u32[]{:S(2)}, u32[]{:S(2)}) collective-permute-start(bf16[128,1024]{1,0:T(8,128)(2,1)} %get-tuple-element.8), channel_id=1, source_target_pairs={{0,0},{2,2},{4,4},{6,6},{8,8},{10,10},{12,12},{14,14},{16,16},{18,... | collective-permute-start | bytes 786440 | tf_op jit(solution)/shard_map/ppermute | solution.py:286
  62.0 31.1 %collective-permute-start.10 = (bf16[4,2,128,256]{3,2,1,0:T(8,128)(2,1)}, bf16[4,2,128,256]{3,2,1,0:T(8,128)(2,1)S(1)}, u32[]{:S(2)}, u32[]{:S(2)}) collective-permute-start(bf16[4,2,128,256]{3,2,1,0:T(8,128)(2,1)} %pack.1.rest_0_), channel_id=1, source_target_pairs={{0,128},{128,0},{1,129},{129,1},{2,130},{130,2},{3,131},{131,3},{4... | collective-permute-start | bytes 1572872 | tf_op jit(solution)/shard_map/ppermute | solution.py:283
  73.4 19.7 %collective-permute-start.11 = (bf16[4,2,128,256]{3,2,1,0:T(8,128)(2,1)S(1)}, bf16[4,2,128,256]{3,2,1,0:T(8,128)(2,1)S(1)}, u32[]{:S(2)}, u32[]{:S(2)}) collective-permute-start(bf16[4,2,128,256]{3,2,1,0:T(8,128)(2,1)S(1)} %collective-permute-done.7.rest_1_), channel_id=1, source_target_pairs={{0,128},{128,0},{1,129},{129,1},{2,130},{130,2},{3,131},{131,3},{4... | collective-permute-start | bytes 1572872 | tf_op jit(solution)/shard_map/ppermute | solution.py:283
  74.2 18.9 %collective-permute-start.12 = (bf16[4,2,128,256]{3,2,1,0:T(8,128)(2,1)S(1)}, bf16[4,2,128,256]{3,2,1,0:T(8,128)(2,1)S(1)}, u32[]{:S(2)}, u32[]{:S(2)}) collective-permute-start(bf16[4,2,128,256]{3,2,1,0:T(8,128)(2,1)S(1)} %collective-permute-done.8.rest_2_), channel_id=1, source_target_pairs={{0,128},{128,0},{1,129},{129,1},{2,130},{130,2},{3,131},{131,3},{4... | collective-permute-start | bytes 1572872 | tf_op jit(solution)/shard_map/ppermute | solution.py:283
  87.5 5.6 %collective-permute-start.13 = (bf16[4,2,128,256]{3,2,1,0:T(8,128)(2,1)S(1)}, bf16[4,2,128,256]{3,2,1,0:T(8,128)(2,1)S(1)}, u32[]{:S(2)}, u32[]{:S(2)}) collective-permute-start(bf16[4,2,128,256]{3,2,1,0:T(8,128)(2,1)S(1)} %collective-permute-done.9.rest_3_), channel_id=1, source_target_pairs={{0,128},{128,0},{1,129},{129,1},{2,130},{130,2},{3,131},{131,3},{4... | collective-permute-start | bytes 1572872 | tf_op jit(solution)/shard_map/ppermute | solution.py:283
  90.6 18.7 %collective-permute-start.15 = (bf16[128,1024]{1,0:T(8,128)(2,1)}, bf16[128,1024]{1,0:T(8,128)(2,1)S(1)}, u32[]{:S(2)}, u32[]{:S(2)}) collective-permute-start(bf16[128,1024]{1,0:T(8,128)(2,1)} %get-tuple-element.9), channel_id=1, source_target_pairs={{0,32},{2,34},{4,36},{6,38},{8,40},{10,42},{12,44},{14,46},{16,48}... | collective-permute-start | bytes 786440 | tf_op jit(solution)/shard_map/ppermute | solution.py:286
  93.1 1.0 copy-start
  97.0 22.9 %collective-permute-start.14 = (bf16[128,1024]{1,0:T(8,128)(2,1)S(1)}, bf16[128,1024]{1,0:T(8,128)(2,1)S(1)}, u32[]{:S(2)}, u32[]{:S(2)}) collective-permute-start(bf16[128,1024]{1,0:T(8,128)(2,1)S(1)} %attend.2), channel_id=1, source_target_pairs={{0,0},{2,2},{4,4},{6,6},{8,8},{10,10},{12,12},{14,14},{16,16},{18,... | collective-permute-start | bytes 786440 | tf_op jit(solution)/shard_map/ppermute | solution.py:302
  116.5 14.8 %collective-permute-start.16 = (bf16[128,1024]{1,0:T(8,128)(2,1)S(1)}, bf16[128,1024]{1,0:T(8,128)(2,1)S(1)}, u32[]{:S(2)}, u32[]{:S(2)}) collective-permute-start(bf16[128,1024]{1,0:T(8,128)(2,1)S(1)} %attend.3), channel_id=1, source_target_pairs={{32,0},{34,2},{36,4},{38,6},{40,8},{42,10},{44,12},{46,14},{48,16}... | collective-permute-start | bytes 786440 | tf_op jit(solution)/shard_map/ppermute | solution.py:302
  132.2 1.1 copy-start.1

commit v2 on v1

--- a/solution.py
+++ b/solution.py
@@ -1,3 +1,4 @@
+import functools
 import math
 
 import jax
@@ -18,10 +19,14 @@
 NT = (((1,), (1,)), ((), ()))
 
 
-def vision_kernel(m_ref, x_ref, w_hbm, gain_ref, ow_hbm, win_ref, send_ref, keep_ref,
-                  w_buf, ow_buf, ctx_ref, part_ref, xp_ref, sems):
-    copies = [pltpu.make_async_copy(w_hbm.at[i], w_buf.at[i], sems.at[i]) for i in range(3)]
-    copies.append(pltpu.make_async_copy(ow_hbm, ow_buf, sems.at[3]))
+def row_of(ref):
+    return jnp.concatenate([ref[n:n + 1] for n in range(ref.shape[0])], axis=1)
+
+
+def vision_kernel(x_ref, w_hbm, gain_ref, ow_hbm, win_ref, send_ref, keep_ref,
+                  w_ref, ow_ref, ctx_ref, part_ref, xp_ref, sems):
+    copies = [pltpu.make_async_copy(w_hbm.at[i], w_ref.at[i], sems.at[i]) for i in range(3)]
+    copies.append(pltpu.make_async_copy(ow_hbm, ow_ref, sems.at[3]))
     for c in copies:
         c.start()
     rows = x_ref.shape[0]
@@ -32,7 +37,7 @@
     xp = jnp.dot(perm, x_ref[...], preferred_element_type=F32)
     xp_ref[...] = xp
     scale = lax.rsqrt(jnp.mean(xp * xp, axis=-1, keepdims=True) + EPSILON)
-    normed = (xp * scale * gain_ref[...]).astype(BF)
+    normed = (xp * scale * row_of(gain_ref)).astype(BF)
     win = jnp.broadcast_to(win_ref[...], (128, rows)).astype(F32).astype(BF)
     win_row = lax.dot_general(win, perm, NT, preferred_element_type=F32)[0:1]
     win_col = lax.dot_general(perm, win, NT, preferred_element_type=F32)[:, 0:1]
@@ -40,7 +45,7 @@
     heads = []
     for n in range(3):
         copies[n].wait()
-        heads.append(jnp.dot(normed, w_buf[n], preferred_element_type=F32).astype(BF))
+        heads.append(jnp.dot(normed, w_ref[n], preferred_element_type=F32).astype(BF))
     q, k, v = heads
     hd = 80
     local = q.shape[1] // hd
@@ -61,23 +66,23 @@
             ctx_ref[:, a:b] = jnp.where(mine, o, ctx_ref[:, a:b] if b - a == 128 else
                                         jnp.concatenate([ctx_ref[:, a:a + 128], o[:, 128:]], axis=1))
     copies[3].wait()
-    part_ref[...] = jnp.dot(ctx_ref[...].astype(BF), ow_buf[...], preferred_element_type=F32)
+    part_ref[...] = jnp.dot(ctx_ref[...].astype(BF), ow_ref[...], preferred_element_type=F32)
     half = rows // 2
-    m = m_ref[0]
+    m = lax.axis_index("mp")
     own = pl.multiple_of(m * half, half)
     other = pl.multiple_of((1 - m) * half, half)
     send_ref[...] = part_ref[pl.ds(other, half), :].astype(BF)
     keep_ref[...] = part_ref[pl.ds(own, half), :] + xp_ref[pl.ds(own, half), :]
 
 
-def vision(m, patches, inner_weight, norm_gain, outer_weight, windows):
+def vision(patches, inner_weight, norm_gain, outer_weight, windows):
     rows, vd = patches.shape
     cols = inner_weight.shape[2]
     vm = pl.BlockSpec(memory_space=pltpu.VMEM)
     hbm = pl.BlockSpec(memory_space=pl.ANY)
     return pl.pallas_call(
         vision_kernel,
-        in_specs=[pl.BlockSpec(memory_space=pltpu.SMEM), vm, hbm, vm, hbm, vm],
+        in_specs=[vm, hbm, vm, hbm, vm],
         out_specs=[vm, vm],
         out_shape=[jax.ShapeDtypeStruct((rows // 2, vd), BF), jax.ShapeDtypeStruct((rows // 2, vd), F32)],
         scratch_shapes=[
@@ -90,12 +95,12 @@
         ],
         cost_estimate=pl.CostEstimate(flops=3 * 10**9, bytes_accessed=8 * 10**6, transcendentals=10**6),
         name="vision",
-    )(m, patches, inner_weight, norm_gain.reshape(1, vd), outer_weight, windows)
+    )(patches, inner_weight, norm_gain.reshape(-1, 128), outer_weight, windows)
 
 
 def merge_kernel(keep_ref, recv_ref, gain_ref, target_ref, out_ref):
     r = keep_ref[...] + recv_ref[...].astype(F32)
-    merged = (r * lax.rsqrt(jnp.mean(r * r, axis=-1, keepdims=True) + EPSILON) * gain_ref[...]).astype(BF)
+    merged = (r * lax.rsqrt(jnp.mean(r * r, axis=-1, keepdims=True) + EPSILON) * row_of(gain_ref)).astype(BF)
     half = r.shape[0] // 2
     w = r.shape[1] // 2
     quarters = jnp.concatenate(
@@ -116,31 +121,34 @@
         in_specs=[vm] * 4,
         out_specs=vm,
         out_shape=jax.ShapeDtypeStruct((slots * 4, keep.shape[1] // 2), BF),
+        compiler_params=pltpu.CompilerParams(vmem_limit_bytes=12 << 20),
         cost_estimate=pl.CostEstimate(flops=4 * 10**8, bytes_accessed=3 * 10**6, transcendentals=10**4),
         name="merge",
-    )(keep, recv, merge_gain.reshape(1, -1), target)
+    )(keep, recv, merge_gain.reshape(-1, 128), target)
 
 
 def place_kernel(in_ref, out_ref):
-    n, w = in_ref.shape
+    n, w = 128, in_ref.shape[1]
     i = lax.broadcasted_iota(jnp.int32, (n, n), 0)
     j = lax.broadcasted_iota(jnp.int32, (n, n), 1)
     quarter = n // 4
     perm = jnp.where(j == 4 * (i & (quarter - 1)) + i // quarter, 1.0, 0.0).astype(BF)
-    y = jnp.dot(perm, in_ref[...], preferred_element_type=F32).astype(BF)
-    for q in range(4):
-        out_ref[:, q * w:(q + 1) * w] = y[q * quarter:(q + 1) * quarter]
+    for b in range(in_ref.shape[0] // n):
+        y = jnp.dot(perm, in_ref[b * n:(b + 1) * n], preferred_element_type=F32).astype(BF)
+        for q in range(4):
+            out_ref[b * quarter:(b + 1) * quarter, q * w:(q + 1) * w] = y[q * quarter:(q + 1) * quarter]
 
 
 def place(arrived):
     n, w = arrived.shape
-    step = 256
+    step = 512
     return pl.pallas_call(
         place_kernel,
         grid=(n // step,),
         in_specs=[pl.BlockSpec((step, w), lambda i: (i, 0))],
         out_specs=pl.BlockSpec((step // 4, 4 * w), lambda i: (i, 0)),
         out_shape=jax.ShapeDtypeStruct((n // 4, 4 * w), BF),
+        compiler_params=pltpu.CompilerParams(vmem_limit_bytes=12 << 20),
         cost_estimate=pl.CostEstimate(flops=4 * 10**8, bytes_accessed=3 * 10**6, transcendentals=0),
         name="place",
     )(arrived)
@@ -161,13 +169,24 @@
     return perm_of(lambda c, z, y, x: (z >> 1 & 1, 2 * (2 * c + (p ^ z >> 2)) + (z & 1), y, x))
 
 
-def attend_kernel(meta_ref, q_ref, *rest):
+def attend_kernel(p, bound_ref, q_ref, *rest):
     near, far = rest[:4], rest[4:8]
-    starts_ref, ends_ref, o_ref, q_scr, m_scr, acc_scr = rest[8:]
-    x, c, here, first = [meta_ref[n] for n in range(4)]
+    o_ref, q_scr, m_scr, acc_scr = rest[8:]
+    c, s = lax.axis_index("section"), lax.axis_index("seq")
+    x = s & 3
+    here = (2 * (p ^ (s >> 4 & 1)) + c) * 4 + (s >> 2 & 3)
+    bounds = [bound_ref[n] for n in range(9)]
+    begin = jnp.int32(0)
+    for b in bounds[:8]:
+        begin = jnp.where(b <= here * QUAD + x * 128, b, begin)
+    first = begin // QUAD
+    lane = lax.broadcasted_iota(jnp.int32, (1, HD), 1)
+    starts = ends = jnp.full((1, HD), 16 * QUAD, jnp.int32)
+    for n in range(8):
+        starts = jnp.where(lane == n, bounds[n], starts)
+        ends = jnp.where(lane == n, bounds[n + 1], ends)
     chips = [x, (x + 3) & 3, (x + 1) & 3, (x + 2) & 3]
-    starts, ends = starts_ref[...], ends_ref[...]
-    chain = q_scr.shape[0] // 2
+    chain = q_scr.shape[0] // 4
 
     def same_doc(base, n):
         at = lax.broadcasted_iota(jnp.int32, (n, HD), 0) + base
@@ -194,7 +213,7 @@
     ahead = jnp.where(j < 128, x, jnp.where(j < 256, chips[1], jnp.where(j < 384, chips[2], chips[3])))
     causal = ahead * 128 + (j & 127) <= x * 128 + (i & 127)
     keys, values = keys_of(here)
-    for g in range(2):
+    for g in range(4):
         part = pl.ds(g * chain, chain)
         s = lax.dot_general(q_scr[part], keys, NT, preferred_element_type=F32)
         s = jnp.where(causal, s, -1e30)
@@ -206,7 +225,7 @@
     @pl.loop(first, here)
     def _(b):
         keys, values = keys_of(b)
-        for g in range(2):
+        for g in range(4):
             part = pl.ds(g * chain, chain)
             s = lax.dot_general(q_scr[part], keys, NT, preferred_element_type=F32)
             old = m_scr[part]
@@ -222,12 +241,12 @@
         o_ref[:, g * 128:(g + 1) * 128] = (acc_scr[part, :HD] / acc_scr[part, HD:]).astype(BF)
 
 
-def attend(meta, query, near, far, starts, ends):
+def attend(p, bounds, query, near, far):
     pieces = [*near, *far]
     vm = pl.BlockSpec(memory_space=pltpu.VMEM)
     return pl.pallas_call(
-        attend_kernel,
-        in_specs=[pl.BlockSpec(memory_space=pltpu.SMEM)] + [vm] * 11,
+        functools.partial(attend_kernel, p),
+        in_specs=[pl.BlockSpec(memory_space=pltpu.SMEM)] + [vm] * 9,
         out_specs=vm,
         out_shape=jax.ShapeDtypeStruct((128, 1024), BF),
         scratch_shapes=[
@@ -238,7 +257,7 @@
         compiler_params=pltpu.CompilerParams(vmem_limit_bytes=32 << 20),
         cost_estimate=pl.CostEstimate(flops=4 * 10**9, bytes_accessed=3 * 10**6, transcendentals=5 * 10**6),
         name="attend",
-    )(meta, query, *pieces, starts, ends)
+    )(bounds, query, *pieces)
 
 
 def pack_kernel(*refs):
@@ -253,16 +272,16 @@
         in_specs=[vm] * len(parts),
         out_specs=vm,
         out_shape=jax.ShapeDtypeStruct((len(parts),) + parts[0].shape, BF),
+        compiler_params=pltpu.CompilerParams(vmem_limit_bytes=8 << 20),
         cost_estimate=pl.CostEstimate(flops=0, bytes_accessed=10**6, transcendentals=0),
         name="pack",
     )(*parts)
 
 
 def context_part(context_query, context_key, context_value, documents):
-    c = lax.axis_index("section")
     s = lax.axis_index("seq")
-    z, y, x = s // (NX * NY), (s // NX) % NY, s % NX
-    a, par = z // 2, z & 1
+    z = s // (NX * NY)
+    a = z // 2
     odd, hi = a & 1, a >> 1
     head = [
         jnp.concatenate([t[:, j * HD:(j + 1) * HD] for t in (context_key, context_value)], axis=1)
@@ -286,19 +305,10 @@
         queries.append(lax.ppermute(
             jnp.where((hi ^ p) == 0, context_query[:, :1024], context_query[:, 1024:]),
             BOTH, quad_move(p)))
-    place = [(2 * (p ^ odd) + c) * 2048 + (s & 15) * 128 for p in range(2)]
-    row_docs = jnp.stack([lax.dynamic_slice_in_dim(documents, t, 1, 0)[0] for t in place])
-    firsts = jnp.sum(documents[None, :] < row_docs[:, None], axis=1).astype(jnp.int32) // QUAD
-    names = jnp.arange(8, dtype=jnp.int32)
-    pad = jnp.full((HD - 8,), 8192, jnp.int32)
-    starts = jnp.sum(documents[None, :] < names[:, None], axis=1).astype(jnp.int32)
-    ends = jnp.sum(documents[None, :] <= names[:, None], axis=1).astype(jnp.int32)
-    starts = jnp.concatenate([starts, pad]).reshape(1, HD)
-    ends = jnp.concatenate([ends, pad]).reshape(1, HD)
+    bounds = jnp.sum(documents[None, :] < jnp.arange(16, dtype=jnp.int32)[:, None], axis=1).astype(jnp.int32)
     back = []
     for p in range(2):
-        meta = jnp.stack([x, c, (2 * (p ^ odd) + c) * 4 + par * 2 + y, firsts[p]]).astype(jnp.int32)
-        o = attend(meta, queries[p], near, far, starts, ends)
+        o = attend(p, bounds, queries[p], near, far)
         back.append(lax.ppermute(o, BOTH, [(t, f) for f, t in quad_move(p)]))
     return jnp.where(hi == 0, jnp.concatenate(back, axis=1), jnp.concatenate(back[::-1], axis=1))
 
@@ -316,15 +326,14 @@
     context_value,
     documents,
 ):
-    m = lax.axis_index("mp").astype(jnp.int32).reshape(1)
-    send, keep = vision(m, patches, inner_weight, norm_gain, outer_weight, windows)
+    send, keep = vision(patches, inner_weight, norm_gain, outer_weight, windows)
     recv = lax.ppermute(send, "mp", [(0, 1), (1, 0)])
     tokens = owners.shape[0]
     target = owners[:, 0]
     order = jnp.arange(tokens, dtype=jnp.int32)
     earlier = (target[:, None] == target[None, :]) & (order[:, None] < order[None, :])
     slot = target * 2 + jnp.sum(earlier, axis=0).astype(jnp.int32)
-    spot = (4 * slot[None, :] + jnp.arange(4, dtype=jnp.int32)[:, None]).reshape(1, 4 * tokens)
+    spot = 4 * jnp.tile(slot[None, :], (1, 4)) + jnp.arange(4 * tokens, dtype=jnp.int32)[None, :] // tokens
     owner_count = lax.axis_size(BOTH)
     outgoing = merge(keep, recv, merge_gain, spot, owner_count * 2)
     arrived = lax.all_to_all(

time: 138 us -> 158 us (1.14)
  the two profiles are of different devices: /device:TPU:113 before, /device:TPU:33 now
where the time goes in v2:
time: 158 us
  waiting for transfers between devices  67.8 us (43%)
  starting transfers between devices  55 us (35%)
  Pallas kernels  31 us (20%)
  local copies, waits for them, and re-layouts  2.02 us (1%)
    ppermute x3, waiting for transfers between devices, context_part(): lax.ppermute(mine, 'seq', [(t, t ^ 8 * d + 4 * e) for t in range(64)])  29.6 us
    pallas_call x2, Pallas kernels, attend(): pl.pallas_call(functools.partial(attend_kernel, p), in_specs=[pl.BlockSpe...  20.2 us
    ppermute x3, waiting for transfers between devices, context_part(): lax.ppermute(near[0], 'seq', [(t, t // 4 * 4 + (t + step) % 4) for t in r...  17.1 us
    all_to_all x1, starting transfers between devices, program(): lax.all_to_all(outgoing.reshape(owner_count, 8, outgoing.shape[1]), BOTH,...  13.3 us
    ppermute x2, starting transfers between devices, context_part(): lax.ppermute(jnp.where(hi ^ p == 0, context_query[:, :1024], context_quer...  9.52 us
    ppermute x2, waiting for transfers between devices, context_part(): back.append(lax.ppermute(o, BOTH, [(t, f) for f, t in quad_move(p)]))  9.25 us
    ppermute x2, starting transfers between devices, context_part(): lax.ppermute(jnp.where(hi ^ p == 0, head[0], head[1]), BOTH, quad_move(p))  8.56 us
    ppermute x2, starting transfers between devices, context_part(): back.append(lax.ppermute(o, BOTH, [(t, f) for f, t in quad_move(p)]))  7.59 us
  transfers between devices with their start and end apart: 18, of which 6 were waited for; matrix products, arithmetic and copies ran while one was open for 1% of the time, Pallas kernels for 19%

profile of v2, /device:TPU:33, one launch (start us, length us, event | category | flops | bytes accessed | tf_op | source)
XLA Modules:
  0.0 158.0 jit_solution(11860767010911956150)
XLA Ops:
  0.7 0.8 fusion.2
  1.5 8.5 %collective-permute-start.2 = (bf16[128,256]{1,0:T(8,128)(2,1)S(1)}, bf16[128,256]{1,0:T(8,128)(2,1)S(1)}, u32[]{:S(2)}, u32[]{:S(2)}) collective-permute-start(bf16[128,256]{1,0:T(8,128)(2,1)S(1)} %get-tuple-element.8), channel_id=1, source_target_pairs={{0,0},{2,2},{4,4},{6,6},{8,8},{10,10},{12,12},{14,14},{16,16},{18,... | collective-permute-start | bytes 196616 | tf_op jit(solution)/shard_map/ppermute | solution.py:292
  10.0 0.1 collective-permute-start.3
  10.1 7.5 %vision.1 = (bf16[128,1280]{1,0:T(8,128)(2,1)}, f32[128,1280]{1,0:T(8,128)}) custom-call(bf16[256,1280]{1,0:T(8,128)(2,1)} %x_ref.1, bf16[3,1280,640]{2,1,0:T(8,128)(2,1)} %w_hbm.1, f32[10,128]{1,0:T(8,128)} %bitcast.12, bf16[640,1280]{1,0:T(8,128)(2,1)} %ow_hbm.1, s32[1,256]{1,0:T(1,128)} %win_ref.1), custom_call_target="tpu_custom_call" | custom-call | flops 3000000000 | bytes 8000000 | tf_op jit(solution)/shard_map/vision/pallas_call | solution.py:83
  17.6 1.4 collective-permute-start
  19.0 0.1 convert_reduce_fusion.1
  19.2 6.0 %collective-permute-done.recv_ref = bf16[128,1280]{1,0:T(8,128)(2,1)S(1)} collective-permute-done((bf16[128,1280]{1,0:T(8,128)(2,1)}, bf16[128,1280]{1,0:T(8,128)(2,1)S(1)}, u32[]{:S(2)}, u32[]{:S(2)}) %collective-permute-start) | collective-permute-done | bytes 327712 | tf_op jit(solution)/shard_map/ppermute | solution.py:330
  25.2 1.1 copy-done
  26.3 1.8 %merge.1 = bf16[1024,640]{1,0:T(8,128)(2,1)} custom-call(f32[128,1280]{1,0:T(8,128)S(1)} %copy-done, bf16[128,1280]{1,0:T(8,128)(2,1)S(1)} %collective-permute-done.recv_ref, f32[10,128]{1,0:T(8,128)S(1)} %bitcast.9, s32[1,256]{1,0:T(1,128)S(1)} %fusion.1.target_ref), custom_call_target="tpu_custom_call" | custom-call | flops 400000000 | bytes 3000000 | tf_op jit(solution)/shard_map/merge/pallas_call | solution.py:119
  28.0 13.3 %all-to-all-start = ((bf16[128,8,640]{2,1,0:T(8,128)(2,1)}), bf16[128,8,640]{2,1,0:T(8,128)(2,1)S(1)}, u32[]{:S(2)}, u32[]{:S(2)}) async-start(bf16[128,8,640]{2,1,0:T(8,128)(2,1)} %bitcast.3), calls=%async_computation | async-start | bytes 2621440 | tf_op jit(solution)/shard_map/all_to_all | solution.py:339
  41.4 2.7 %collective-permute-start.6 = (bf16[2,128,256]{2,1,0:T(8,128)(2,1)S(1)}, bf16[2,128,256]{2,1,0:T(8,128)(2,1)S(1)}, u32[]{:S(2)}, u32[]{:S(2)}) collective-permute-start(bf16[2,128,256]{2,1,0:T(8,128)(2,1)S(1)} %maximum_select_fusion.1.refs_0_), channel_id=1, source_target_pairs={{0,24},{2,26},{4,28},{6,30},{8,16},{10,18},{12,20},{14,22},{16,8},... | collective-permute-start | bytes 393224 | tf_op jit(solution)/shard_map/ppermute | solution.py:296
  44.2 1.2 collective-permute-start.5
  45.4 0.3 collective-permute-start.4
  45.7 29.6 %collective-permute-done.6.refs_3_ = bf16[2,128,256]{2,1,0:T(8,128)(2,1)S(1)} collective-permute-done((bf16[2,128,256]{2,1,0:T(8,128)(2,1)S(1)}, bf16[2,128,256]{2,1,0:T(8,128)(2,1)S(1)}, u32[]{:S(2)}, u32[]{:S(2)}) %collective-permute-start.6) | collective-permute-done | bytes 131104 | tf_op jit(solution)/shard_map/ppermute | solution.py:296
  75.3 3.1 %collective-permute-start.9 = (bf16[4,2,128,256]{3,2,1,0:T(8,128)(2,1)S(1)}, bf16[4,2,128,256]{3,2,1,0:T(8,128)(2,1)S(1)}, u32[]{:S(2)}, u32[]{:S(2)}) collective-permute-start(bf16[4,2,128,256]{3,2,1,0:T(8,128)(2,1)S(1)} %pack.1.rest_0_), channel_id=1, source_target_pairs={{0,4},{2,6},{4,0},{6,2},{8,12},{10,14},{12,8},{14,10},{16,20},{18,... | collective-permute-start | bytes 1572872 | tf_op jit(solution)/shard_map/ppermute | solution.py:299
  78.4 0.9 collective-permute-start.8
  79.4 0.5 collective-permute-start.7
  79.9 1.5 collective-permute-start.10
  81.4 8.3 %collective-permute-done.9.rest_3_ = bf16[4,2,128,256]{3,2,1,0:T(8,128)(2,1)S(1)} collective-permute-done((bf16[4,2,128,256]{3,2,1,0:T(8,128)(2,1)S(1)}, bf16[4,2,128,256]{3,2,1,0:T(8,128)(2,1)S(1)}, u32[]{:S(2)}, u32[]{:S(2)}) %collective-permute-start.9) | collective-permute-done | bytes 524320 | tf_op jit(solution)/shard_map/ppermute | solution.py:299
  89.7 2.9 %collective-permute-start.13 = (bf16[4,2,128,256]{3,2,1,0:T(8,128)(2,1)S(1)}, bf16[4,2,128,256]{3,2,1,0:T(8,128)(2,1)S(1)}, u32[]{:S(2)}, u32[]{:S(2)}) collective-permute-start(bf16[4,2,128,256]{3,2,1,0:T(8,128)(2,1)S(1)} %collective-permute-done.9.rest_3_), channel_id=1, source_target_pairs={{0,128},{128,0},{1,129},{129,1},{2,130},{130,2},{3,131},{131,3},{4... | collective-permute-start | bytes 1572872 | tf_op jit(solution)/shard_map/ppermute | solution.py:302
  92.6 8.8 %collective-permute-done.8.rest_2_ = bf16[4,2,128,256]{3,2,1,0:T(8,128)(2,1)S(1)} collective-permute-done((bf16[4,2,128,256]{3,2,1,0:T(8,128)(2,1)S(1)}, bf16[4,2,128,256]{3,2,1,0:T(8,128)(2,1)S(1)}, u32[]{:S(2)}, u32[]{:S(2)}) %collective-permute-start.8) | collective-permute-done | bytes 524320 | tf_op jit(solution)/shard_map/ppermute | solution.py:299
  101.4 1.5 collective-permute-start.12
  103.0 7.7 %collective-permute-start.1 = (bf16[128,1024]{1,0:T(8,128)(2,1)S(1)}, bf16[128,1024]{1,0:T(8,128)(2,1)S(1)}, u32[]{:S(2)}, u32[]{:S(2)}) collective-permute-start(bf16[128,1024]{1,0:T(8,128)(2,1)S(1)} %get-tuple-element.6), channel_id=1, source_target_pairs={{0,0},{2,2},{4,4},{6,6},{8,8},{10,10},{12,12},{14,14},{16,16},{18,... | collective-permute-start | bytes 786440 | tf_op jit(solution)/shard_map/ppermute | solution.py:305
  110.7 0.2 convert_reduce_fusion.bound_ref
  110.9 5.8 %collective-permute-done.1.q_ref = bf16[128,1024]{1,0:T(8,128)(2,1)S(1)} collective-permute-done((bf16[128,1024]{1,0:T(8,128)(2,1)S(1)}, bf16[128,1024]{1,0:T(8,128)(2,1)S(1)}, u32[]{:S(2)}, u32[]{:S(2)}) %collective-permute-start.1) | collective-permute-done | bytes 262176 | tf_op jit(solution)/shard_map/ppermute | solution.py:305
  116.7 1.8 %collective-permute-start.15 = (bf16[128,1024]{1,0:T(8,128)(2,1)S(1)}, bf16[128,1024]{1,0:T(8,128)(2,1)S(1)}, u32[]{:S(2)}, u32[]{:S(2)}) collective-permute-start(bf16[128,1024]{1,0:T(8,128)(2,1)S(1)} %get-tuple-element.7), channel_id=1, source_target_pairs={{0,32},{2,34},{4,36},{6,38},{8,40},{10,42},{12,44},{14,46},{16,48}... | collective-permute-start | bytes 786440 | tf_op jit(solution)/shard_map/ppermute | solution.py:305
  118.5 5.9 %attend.2 = bf16[128,1024]{1,0:T(8,128)(2,1)S(1)} custom-call(s32[16]{0:T(128)S(1)} %convert_reduce_fusion.bound_ref, bf16[128,1024]{1,0:T(8,128)(2,1)S(1)} %collective-permute-done.1.q_ref, bf16[4,2,128,256]{3,2,1,0:T(8,128)(2,1)S(1)} %pack.1.rest_0_, bf16[4,2,128,256]{3,2,1,0:T(8,128)(2,1)S(1)} %collective-permute-done.7.rest_1_, ...), custom_call_target="tpu_custom_call" | custom-call | flops 4000000000 | bytes 3000000 | tf_op jit(solution)/shard_map/attend/pallas_call | solution.py:247
  124.4 7.5 %collective-permute-start.14 = (bf16[128,1024]{1,0:T(8,128)(2,1)S(1)}, bf16[128,1024]{1,0:T(8,128)(2,1)S(1)}, u32[]{:S(2)}, u32[]{:S(2)}) collective-permute-start(bf16[128,1024]{1,0:T(8,128)(2,1)S(1)} %attend.2), channel_id=1, source_target_pairs={{0,0},{2,2},{4,4},{6,6},{8,8},{10,10},{12,12},{14,14},{16,16},{18,... | collective-permute-start | bytes 786440 | tf_op jit(solution)/shard_map/ppermute | solution.py:312
  131.9 14.3 %attend.3 = bf16[128,1024]{1,0:T(8,128)(2,1)S(1)} custom-call(s32[16]{0:T(128)S(1)} %convert_reduce_fusion.bound_ref, bf16[128,1024]{1,0:T(8,128)(2,1)S(1)} %collective-permute-done.15.q_ref, bf16[4,2,128,256]{3,2,1,0:T(8,128)(2,1)S(1)} %pack.1.rest_0_, bf16[4,2,128,256]{3,2,1,0:T(8,128)(2,1)S(1)} %collective-permute-done.7.rest_1_, ...), custom_call_target="tpu_custom_call" | custom-call | flops 4000000000 | bytes 3000000 | tf_op jit(solution)/shard_map/attend/pallas_call | solution.py:247
  146.3 9.2 %collective-permute-done.16 = bf16[128,1024]{1,0:T(8,128)(2,1)S(1)} collective-permute-done((bf16[128,1024]{1,0:T(8,128)(2,1)S(1)}, bf16[128,1024]{1,0:T(8,128)(2,1)S(1)}, u32[]{:S(2)}, u32[]{:S(2)}) %collective-permute-start.16) | collective-permute-done | bytes 262176 | tf_op jit(solution)/shard_map/ppermute | solution.py:312
  155.6 0.9 maximum_select_fusion
  156.5 1.5 place.1
  (31 shorter events, 0.4 us)
Async XLA Ops:
  1.5 39.8 %collective-permute-start.2 = (bf16[128,256]{1,0:T(8,128)(2,1)S(1)}, bf16[128,256]{1,0:T(8,128)(2,1)S(1)}, u32[]{:S(2)}, u32[]{:S(2)}) collective-permute-start(bf16[128,256]{1,0:T(8,128)(2,1)S(1)} %get-tuple-element.8), channel_id=1, source_target_pairs={{0,0},{2,2},{4,4},{6,6},{8,8},{10,10},{12,12},{14,14},{16,16},{18,... | collective-permute-start | bytes 196616 | tf_op jit(solution)/shard_map/ppermute | solution.py:292
  10.0 31.4 %collective-permute-start.3 = (bf16[128,256]{1,0:T(8,128)(2,1)S(1)}, bf16[128,256]{1,0:T(8,128)(2,1)S(1)}, u32[]{:S(2)}, u32[]{:S(2)}) collective-permute-start(bf16[128,256]{1,0:T(8,128)(2,1)S(1)} %get-tuple-element.9), channel_id=1, source_target_pairs={{0,32},{2,34},{4,36},{6,38},{8,40},{10,42},{12,44},{14,46},{16,48}... | collective-permute-start | bytes 196616 | tf_op jit(solution)/shard_map/ppermute | solution.py:292
  10.1 8.9 %copy-start.4 = (s32[64,1]{0,1:T(1,128)S(1)}, s32[64,1]{0,1:T(1,128)}, u32[]{:S(2)}) copy-start(s32[64,1]{0,1:T(1,128)} %param.17) | copy-start | bytes 772
  10.1 15.1 %copy-start.1 = (f32[1280]{0:T(1024)S(1)}, f32[1280]{0:T(1024)}, u32[]{:S(2)}) copy-start(f32[1280]{0:T(1024)} %param.15) | copy-start | bytes 15364
  17.6 7.6 %collective-permute-start = (bf16[128,1280]{1,0:T(8,128)(2,1)}, bf16[128,1280]{1,0:T(8,128)(2,1)S(1)}, u32[]{:S(2)}, u32[]{:S(2)}) collective-permute-start(bf16[128,1280]{1,0:T(8,128)(2,1)} %get-tuple-element.5), channel_id=1, source_target_pairs={{0,1},{1,0},{2,3},{3,2},{4,5},{5,4},{6,7},{7,6},{8,9},{9,8},{10,11... | collective-permute-start | bytes 983048 | tf_op jit(solution)/shard_map/ppermute | solution.py:330
  25.2 1.1 copy-start
  28.0 128.5 %all-to-all-start = ((bf16[128,8,640]{2,1,0:T(8,128)(2,1)}), bf16[128,8,640]{2,1,0:T(8,128)(2,1)S(1)}, u32[]{:S(2)}, u32[]{:S(2)}) async-start(bf16[128,8,640]{2,1,0:T(8,128)(2,1)} %bitcast.3), calls=%async_computation | async-start | bytes 2621440 | tf_op jit(solution)/shard_map/all_to_all | solution.py:339
  41.3 61.6 %copy-start.2 = (bf16[128,2048]{1,0:T(8,128)(2,1)S(1)}, bf16[128,2048]{1,0:T(8,128)(2,1)}, u32[]{:S(2)}) copy-start(bf16[128,2048]{1,0:T(8,128)(2,1)} %param.18) | copy-start | bytes 1572868
  41.4 69.3 %copy-start.3 = (s32[8192]{0:T(1024)S(1)}, s32[8192]{0:T(1024)}, u32[]{:S(2)}) copy-start(s32[8192]{0:T(1024)} %param.21) | copy-start | bytes 98308
  41.4 33.8 %collective-permute-start.6 = (bf16[2,128,256]{2,1,0:T(8,128)(2,1)S(1)}, bf16[2,128,256]{2,1,0:T(8,128)(2,1)S(1)}, u32[]{:S(2)}, u32[]{:S(2)}) collective-permute-start(bf16[2,128,256]{2,1,0:T(8,128)(2,1)S(1)} %maximum_select_fusion.1.refs_0_), channel_id=1, source_target_pairs={{0,24},{2,26},{4,28},{6,30},{8,16},{10,18},{12,20},{14,22},{16,8},... | collective-permute-start | bytes 393224 | tf_op jit(solution)/shard_map/ppermute | solution.py:296
  44.2 31.1 %collective-permute-start.5 = (bf16[2,128,256]{2,1,0:T(8,128)(2,1)S(1)}, bf16[2,128,256]{2,1,0:T(8,128)(2,1)S(1)}, u32[]{:S(2)}, u32[]{:S(2)}) collective-permute-start(bf16[2,128,256]{2,1,0:T(8,128)(2,1)S(1)} %maximum_select_fusion.1.refs_0_), channel_id=1, source_target_pairs={{0,16},{2,18},{4,20},{6,22},{8,24},{10,26},{12,28},{14,30},{16,0},... | collective-permute-start | bytes 393224 | tf_op jit(solution)/shard_map/ppermute | solution.py:296
  45.4 29.9 %collective-permute-start.4 = (bf16[2,128,256]{2,1,0:T(8,128)(2,1)S(1)}, bf16[2,128,256]{2,1,0:T(8,128)(2,1)S(1)}, u32[]{:S(2)}, u32[]{:S(2)}) collective-permute-start(bf16[2,128,256]{2,1,0:T(8,128)(2,1)S(1)} %maximum_select_fusion.1.refs_0_), channel_id=1, source_target_pairs={{0,8},{2,10},{4,12},{6,14},{8,0},{10,2},{12,4},{14,6},{16,24},{18,... | collective-permute-start | bytes 393224 | tf_op jit(solution)/shard_map/ppermute | solution.py:296
  75.3 14.4 %collective-permute-start.9 = (bf16[4,2,128,256]{3,2,1,0:T(8,128)(2,1)S(1)}, bf16[4,2,128,256]{3,2,1,0:T(8,128)(2,1)S(1)}, u32[]{:S(2)}, u32[]{:S(2)}) collective-permute-start(bf16[4,2,128,256]{3,2,1,0:T(8,128)(2,1)S(1)} %pack.1.rest_0_), channel_id=1, source_target_pairs={{0,4},{2,6},{4,0},{6,2},{8,12},{10,14},{12,8},{14,10},{16,20},{18,... | collective-permute-start | bytes 1572872 | tf_op jit(solution)/shard_map/ppermute | solution.py:299
  78.4 23.0 %collective-permute-start.8 = (bf16[4,2,128,256]{3,2,1,0:T(8,128)(2,1)S(1)}, bf16[4,2,128,256]{3,2,1,0:T(8,128)(2,1)S(1)}, u32[]{:S(2)}, u32[]{:S(2)}) collective-permute-start(bf16[4,2,128,256]{3,2,1,0:T(8,128)(2,1)S(1)} %pack.1.rest_0_), channel_id=1, source_target_pairs={{0,6},{2,0},{4,2},{6,4},{8,14},{10,8},{12,10},{14,12},{16,22},{18,... | collective-permute-start | bytes 1572872 | tf_op jit(solution)/shard_map/ppermute | solution.py:299
  79.4 23.5 %collective-permute-start.7 = (bf16[4,2,128,256]{3,2,1,0:T(8,128)(2,1)S(1)}, bf16[4,2,128,256]{3,2,1,0:T(8,128)(2,1)S(1)}, u32[]{:S(2)}, u32[]{:S(2)}) collective-permute-start(bf16[4,2,128,256]{3,2,1,0:T(8,128)(2,1)S(1)} %pack.1.rest_0_), channel_id=1, source_target_pairs={{0,2},{2,4},{4,6},{6,0},{8,10},{10,12},{12,14},{14,8},{16,18},{18,... | collective-permute-start | bytes 1572872 | tf_op jit(solution)/shard_map/ppermute | solution.py:299
  79.9 38.6 %collective-permute-start.10 = (bf16[4,2,128,256]{3,2,1,0:T(8,128)(2,1)S(1)}, bf16[4,2,128,256]{3,2,1,0:T(8,128)(2,1)S(1)}, u32[]{:S(2)}, u32[]{:S(2)}) collective-permute-start(bf16[4,2,128,256]{3,2,1,0:T(8,128)(2,1)S(1)} %pack.1.rest_0_), channel_id=1, source_target_pairs={{0,128},{128,0},{1,129},{129,1},{2,130},{130,2},{3,131},{131,3},{4... | collective-permute-start | bytes 1572872 | tf_op jit(solution)/shard_map/ppermute | solution.py:302
  89.7 28.8 %collective-permute-start.13 = (bf16[4,2,128,256]{3,2,1,0:T(8,128)(2,1)S(1)}, bf16[4,2,128,256]{3,2,1,0:T(8,128)(2,1)S(1)}, u32[]{:S(2)}, u32[]{:S(2)}) collective-permute-start(bf16[4,2,128,256]{3,2,1,0:T(8,128)(2,1)S(1)} %collective-permute-done.9.rest_3_), channel_id=1, source_target_pairs={{0,128},{128,0},{1,129},{129,1},{2,130},{130,2},{3,131},{131,3},{4... | collective-permute-start | bytes 1572872 | tf_op jit(solution)/shard_map/ppermute | solution.py:302
  101.4 17.1 %collective-permute-start.12 = (bf16[4,2,128,256]{3,2,1,0:T(8,128)(2,1)S(1)}, bf16[4,2,128,256]{3,2,1,0:T(8,128)(2,1)S(1)}, u32[]{:S(2)}, u32[]{:S(2)}) collective-permute-start(bf16[4,2,128,256]{3,2,1,0:T(8,128)(2,1)S(1)} %collective-permute-done.8.rest_2_), channel_id=1, source_target_pairs={{0,128},{128,0},{1,129},{129,1},{2,130},{130,2},{3,131},{131,3},{4... | collective-permute-start | bytes 1572872 | tf_op jit(solution)/shard_map/ppermute | solution.py:302
  102.9 15.6 %collective-permute-start.11 = (bf16[4,2,128,256]{3,2,1,0:T(8,128)(2,1)S(1)}, bf16[4,2,128,256]{3,2,1,0:T(8,128)(2,1)S(1)}, u32[]{:S(2)}, u32[]{:S(2)}) collective-permute-start(bf16[4,2,128,256]{3,2,1,0:T(8,128)(2,1)S(1)} %collective-permute-done.7.rest_1_), channel_id=1, source_target_pairs={{0,128},{128,0},{1,129},{129,1},{2,130},{130,2},{3,131},{131,3},{4... | collective-permute-start | bytes 1572872 | tf_op jit(solution)/shard_map/ppermute | solution.py:302
  103.0 13.7 %collective-permute-start.1 = (bf16[128,1024]{1,0:T(8,128)(2,1)S(1)}, bf16[128,1024]{1,0:T(8,128)(2,1)S(1)}, u32[]{:S(2)}, u32[]{:S(2)}) collective-permute-start(bf16[128,1024]{1,0:T(8,128)(2,1)S(1)} %get-tuple-element.6), channel_id=1, source_target_pairs={{0,0},{2,2},{4,4},{6,6},{8,8},{10,10},{12,12},{14,14},{16,16},{18,... | collective-permute-start | bytes 786440 | tf_op jit(solution)/shard_map/ppermute | solution.py:305
  116.7 15.2 %collective-permute-start.15 = (bf16[128,1024]{1,0:T(8,128)(2,1)S(1)}, bf16[128,1024]{1,0:T(8,128)(2,1)S(1)}, u32[]{:S(2)}, u32[]{:S(2)}) collective-permute-start(bf16[128,1024]{1,0:T(8,128)(2,1)S(1)} %get-tuple-element.7), channel_id=1, source_target_pairs={{0,32},{2,34},{4,36},{6,38},{8,40},{10,42},{12,44},{14,46},{16,48}... | collective-permute-start | bytes 786440 | tf_op jit(solution)/shard_map/ppermute | solution.py:305
  124.4 21.9 %collective-permute-start.14 = (bf16[128,1024]{1,0:T(8,128)(2,1)S(1)}, bf16[128,1024]{1,0:T(8,128)(2,1)S(1)}, u32[]{:S(2)}, u32[]{:S(2)}) collective-permute-start(bf16[128,1024]{1,0:T(8,128)(2,1)S(1)} %attend.2), channel_id=1, source_target_pairs={{0,0},{2,2},{4,4},{6,6},{8,8},{10,10},{12,12},{14,14},{16,16},{18,... | collective-permute-start | bytes 786440 | tf_op jit(solution)/shard_map/ppermute | solution.py:312
  146.2 9.3 %collective-permute-start.16 = (bf16[128,1024]{1,0:T(8,128)(2,1)S(1)}, bf16[128,1024]{1,0:T(8,128)(2,1)S(1)}, u32[]{:S(2)}, u32[]{:S(2)}) collective-permute-start(bf16[128,1024]{1,0:T(8,128)(2,1)S(1)} %attend.3), channel_id=1, source_target_pairs={{32,0},{34,2},{36,4},{38,6},{40,8},{42,10},{44,12},{46,14},{48,16}... | collective-permute-start | bytes 786440 | tf_op jit(solution)/shard_map/ppermute | solution.py:312
